TPU v7x, 32 devices: a whole 2x2x4 slice. The times are simulated.
32 devices in a mesh: face: 8 (over y, x, core), member: 4 (over z).
Axes of the slice: x: 2, y: 2, z: 4, core: 2. Of those that a mesh axis runs over, the one named last changes fastest.
Arguments:
- features: bfloat16 [8, 48, 16, 16, 256], P('member', 'face'), may hold values from -6 to 6
- observed: bfloat16 [48, 80, 256], P('face', None, 'member'), may hold values from -6 to 6
- conv_weights: bfloat16 [2304, 2, 256], P(('face', 'member')), may hold values from -0.125 to 0.125
- head_weight: bfloat16 [256, 80], P(('face', 'member')), may hold values from -0.375 to 0.375
- adjacency: int32 [48, 4, 3], replicated, may hold values from 0 to 47, as said below
- placement_map: int32 [48], replicated, may hold values from 0 to 47, each once
Outputs:
- conv_grads: float32 [2304, 2, 256], P(('face', 'member'))
- head_grad: float32 [256, 80], P(('face', 'member'))
Inputs may be any that keep to these rules, and one draw needn't show every extreme that they name: `adjacency`: the table is the gluing of the 12 HEALPix base faces, each cut into 4 square tiles, under a labelling of the tiles drawn from the seed: entry [t, a] = (n, b, f) glues side a of tile t to side b of tile n, reversed when f is 1; the gluing is mutual (entry [n, b] is (t, a, f)) and never joins a side to itself. `placement_map`: each tile stands at exactly one slot.
All inputs are finite; a program needn't handle non-finite values.
Results may differ from a plain program's by a relative error of at most 0.0005.
Values may be sent and summed in bfloat16 or wider, within the bound.
A program may use at most 128 MiB of HBM per device.

v0:
```python
import jax
import jax.numpy as jnp
from jax import lax
from jax.sharding import PartitionSpec as P

smooth_sq = 0.0625


def split_edges(grid_field):
    return jnp.stack(
        [
            grid_field[:, :, 0],
            grid_field[:, :, :, -1],
            grid_field[:, :, -1],
            grid_field[:, :, :, 0],
        ],
        axis=2,
    )


def border_of(padded):
    return jnp.stack(
        [
            padded[:, :, 0, 1:-1],
            padded[:, :, 1:-1, -1],
            padded[:, :, -1, 1:-1],
            padded[:, :, 1:-1, 0],
        ],
        axis=2,
    )


def surround(grid_field, border):
    ensemble_members, tile_count, height, tile_w, channels = grid_field.shape
    corner = jnp.zeros((ensemble_members, tile_count, 1, 1, channels), grid_field.dtype)
    top_row = jnp.concatenate([corner, border[:, :, 0][:, :, None], corner], axis=3)
    low_row = jnp.concatenate([corner, border[:, :, 2][:, :, None], corner], axis=3)
    middle = jnp.concatenate(
        [border[:, :, 3][:, :, :, None], grid_field, border[:, :, 1][:, :, :, None]], axis=3
    )
    return jnp.concatenate([top_row, middle, low_row], axis=2)


def convolve(padded, weight):
    channels = weight.shape[1]
    height = padded.shape[2] - 2
    tile_w = padded.shape[3] - 2
    summed = None
    for tap_index in range(9):
        row_off, col_off = divmod(tap_index, 3)
        window = padded[:, :, row_off : row_off + height, col_off : col_off + tile_w, :]
        product_part = jnp.dot(
            window.reshape(-1, channels),
            weight[tap_index * channels : (tap_index + 1) * channels],
            preferred_element_type=jnp.float32,
        )
        summed = product_part if summed is None else summed + product_part
    return summed.reshape(padded.shape[:2] + (height, tile_w, channels))


def transpose_conv(slope_in, weight):
    channels = weight.shape[1]
    ensemble_members, tile_count, height, tile_w, _ = slope_in.shape
    result = jnp.zeros(
        (ensemble_members, tile_count, height + 2, tile_w + 2, channels), jnp.float32
    )
    flat_slope = slope_in.reshape(-1, channels)
    for tap_index in range(9):
        row_off, col_off = divmod(tap_index, 3)
        product_part = lax.dot_general(
            flat_slope,
            weight[tap_index * channels : (tap_index + 1) * channels],
            (((1,), (1,)), ((), ())),
            preferred_element_type=jnp.float32,
        )
        result = result.at[:, :, row_off : row_off + height, col_off : col_off + tile_w, :].add(
            product_part.reshape(slope_in.shape)
        )
    return result


def weight_slope(padded, slope_in):
    channels = slope_in.shape[-1]
    height = slope_in.shape[2]
    tile_w = slope_in.shape[3]
    flat_slope = slope_in.reshape(-1, channels)
    pieces_out = []
    for tap_index in range(9):
        row_off, col_off = divmod(tap_index, 3)
        window = padded[:, :, row_off : row_off + height, col_off : col_off + tile_w, :]
        pieces_out.append(
            lax.dot_general(
                window.reshape(-1, channels),
                flat_slope,
                (((0,), (0,)), ((), ())),
                preferred_element_type=jnp.float32,
            )
        )
    return jnp.concatenate(pieces_out, axis=0)


def dsilu(argument):
    sigmoid_v = jax.nn.sigmoid(argument)
    return sigmoid_v * (1.0 + argument * (1.0 - sigmoid_v))


def partner_table(adjacency, placement_map, first_slot, tile_dev):
    tile_count = placement_map.shape[0]
    slot_ids = jnp.arange(tile_count, dtype=jnp.int32)
    my_slots = first_slot + jnp.arange(tile_dev, dtype=jnp.int32)
    slot_hit = (slot_ids[None, :] == my_slots[:, None]).astype(jnp.int32)
    my_tiles = jnp.sum(slot_hit * placement_map[None, :], axis=1)
    tile_hit = (slot_ids[None, :] == my_tiles[:, None]).astype(jnp.int32)
    entries = jnp.sum(tile_hit[:, :, None, None] * adjacency[None], axis=1)
    slot_of = jnp.sum(
        slot_ids[:, None] * (placement_map[:, None] == slot_ids[None, :]).astype(jnp.int32), axis=0
    )
    source_slot = jnp.sum(
        (slot_ids[None, None, :] == entries[:, :, 0][:, :, None]).astype(jnp.int32)
        * slot_of[None, None, :],
        axis=2,
    )
    source_index = source_slot * 4 + entries[:, :, 1]
    edge_ids = jnp.arange(tile_count * 4, dtype=jnp.int32)
    selector = (edge_ids[None, None, :] == source_index[:, :, None]).astype(jnp.bfloat16)
    return (selector, entries[:, :, 2])


def fetch_rims(gathered, selector, flip_flags, tile_dev):
    ensemble_members, tile_count, side_count, length, channels = gathered.shape
    flattened = gathered.reshape(ensemble_members, tile_count * side_count, length * channels)
    fetched = jnp.einsum("abe,mef->mabf", selector, flattened, preferred_element_type=jnp.float32)
    fetched = fetched.astype(jnp.bfloat16).reshape(
        ensemble_members, tile_dev, side_count, length, channels
    )
    return jnp.where(flip_flags[None, :, :, None, None] == 1, fetched[:, :, :, ::-1, :], fetched)


def score_slope(local_vals, all_vals, obs_vals, height):
    ensemble_members = all_vals.shape[0]
    spread = local_vals[:, None] - all_vals[None]
    paired = jnp.sum(spread * lax.rsqrt(spread * spread + smooth_sq), axis=1)
    own_gap = local_vals - obs_vals[None]
    return (
        own_gap * lax.rsqrt(own_gap * own_gap + smooth_sq) / ensemble_members
        - paired / (ensemble_members * ensemble_members)
    ) / height


def shards(features, observed, conv_weights, head_weight, adjacency, placement_map):
    members, tile_dev, height, tile_w, channels = features.shape
    full_weights, full_head = (
        lax.all_gather(conv_weights, ("face", "member"), axis=0, tiled=True),
        lax.all_gather(head_weight, ("face", "member"), axis=0, tiled=True),
    )
    selector, flip_flags = partner_table(
        adjacency, placement_map, lax.axis_index("face") * tile_dev, tile_dev
    )
    feature_edges = lax.all_gather(split_edges(features), "face", axis=1, tiled=True)
    pad_in = surround(features, fetch_rims(feature_edges, selector, flip_flags, tile_dev))
    pre_one = convolve(pad_in, full_weights[:, 0, :])
    act_one = jax.nn.silu(pre_one).astype(jnp.bfloat16)
    hidden_edges = lax.all_gather(split_edges(act_one), "face", axis=1, tiled=True)
    pad_mid = surround(act_one, fetch_rims(hidden_edges, selector, flip_flags, tile_dev))
    pre_two = convolve(pad_mid, full_weights[:, 1, :])
    act_two = jax.nn.silu(pre_two).astype(jnp.bfloat16)
    flat_two = act_two.reshape(members, tile_dev, height * tile_w, channels)
    outputs = jnp.einsum(
        "mtpc,cv->mtvp", flat_two, full_head, preferred_element_type=jnp.float32
    ).astype(jnp.bfloat16)
    by_pixel = lax.all_to_all(outputs, "member", split_axis=3, concat_axis=0, tiled=True)
    pixel_vals = by_pixel.astype(jnp.float32)
    slope_cells = score_slope(pixel_vals, pixel_vals, observed.astype(jnp.float32), height).astype(
        jnp.bfloat16
    )
    slope_out = lax.all_to_all(slope_cells, "member", split_axis=0, concat_axis=3, tiled=True)
    head_term = jnp.einsum("mtpc,mtvp->cv", flat_two, slope_out, preferred_element_type=jnp.float32)
    back_two = jnp.einsum("mtvp,cv->mtpc", slope_out, full_head, preferred_element_type=jnp.float32)
    back_two = back_two.reshape(members, tile_dev, height, tile_w, channels)
    slope_two = (back_two * dsilu(pre_two)).astype(jnp.bfloat16)
    grad_two = weight_slope(pad_mid, slope_two)
    late_shard, head_shard = (
        lax.psum_scatter(grad_two, ("face", "member"), scatter_dimension=0, tiled=True),
        lax.psum_scatter(head_term, ("face", "member"), scatter_dimension=0, tiled=True),
    )
    pad_slope = transpose_conv(slope_two, full_weights[:, 1, :]).astype(jnp.bfloat16)
    rim_edges = lax.all_gather(border_of(pad_slope), "face", axis=1, tiled=True)
    returned = fetch_rims(rim_edges, selector, flip_flags, tile_dev).astype(jnp.float32)
    slope_mid = pad_slope[:, :, 1:-1, 1:-1].astype(jnp.float32)
    slope_mid = slope_mid.at[:, :, 0].add(returned[:, :, 0])
    slope_mid = slope_mid.at[:, :, :, -1].add(returned[:, :, 1])
    slope_mid = slope_mid.at[:, :, -1].add(returned[:, :, 2])
    slope_mid = slope_mid.at[:, :, :, 0].add(returned[:, :, 3])
    slope_one = (slope_mid * dsilu(pre_one)).astype(jnp.bfloat16)
    grad_one = weight_slope(pad_in, slope_one)
    early_shard = lax.psum_scatter(grad_one, ("face", "member"), scatter_dimension=0, tiled=True)
    conv_shard = jnp.stack([early_shard, late_shard], axis=1)
    return (conv_shard, head_shard)


def solution(mesh):
    in_specs = (
        P("member", "face", None, None, None),
        P("face", None, "member"),
        P(("face", "member"), None, None),
        P(("face", "member"), None),
        P(),
        P(),
    )
    out_specs = (P(("face", "member"), None, None), P(("face", "member"), None))
    return jax.shard_map(shards, mesh=mesh, in_specs=in_specs, out_specs=out_specs, check_vma=False)
```

profile of v0, /device:TPU:0, one launch (start us, length us, event | category | flops | bytes accessed | tf_op | source)
XLA Modules:
  0.0 850.0 jit_solution(15067462551593991296)
XLA Ops:
  7.2 1.8 fusion.111
  13.3 32.6 %all-gather.5.cloned.1.call-done = bf16[2,48,4,16,256]{4,3,1,0,2:T(8,128)(2,1)} async-done(((bf16[2,6,4,16,256]{4,3,1,0,2:T(8,128)(2,1)}), bf16[2,48,4,16,256]{4,3,1,0,2:T(8,128)(2,1)}) %all-gather.5.cloned.1.call-update) | async-done | bytes 3145744 | tf_op jit(solution)/shard_map/all_gather | solution.py:159
  45.9 2.3 copy.300
  48.3 3.4 reshape.811
  51.7 2.6 fusion.3
  57.0 2.9 pad_maximum_fusion.4
  60.0 3.6 pad_maximum_fusion
  63.6 3.6 fusion.108
  67.3 3.2 fusion.107
  70.5 36.2 %all-gather.7.cloned.1.call-done = bf16[2304,2,256]{2,0,1:T(8,128)(2,1)} async-done(((bf16[72,2,256]{2,0,1:T(8,128)(2,1)}), bf16[2304,2,256]{2,0,1:T(8,128)(2,1)}) %all-gather.7.cloned.1.call-update) | async-done | bytes 2359312 | tf_op jit(solution)/shard_map/all_gather | solution.py:153
  106.7 2.1 fusion.32
  110.4 1.6 convolution_add_fusion.14
  115.0 1.6 convolution_add_fusion.11
  118.3 1.6 convolution_add_fusion.9
  124.4 67.0 %all_gather.18 = bf16[256,80]{1,0:T(8,128)(2,1)S(1)} all-gather(bf16[8,80]{1,0:T(8,128)(2,1)S(1)} %copy-done.36), channel_id=1, replica_groups=mesh['face'=8,'member'=4] {'face','member'}, dimensions={0}, use_global_device_ids=true | all-gather | bytes 42240 | tf_op jit(solution)/shard_map/all_gather | solution.py:154
  191.4 6.1 reshape.813
  197.5 2.6 fusion.4
  204.4 3.9 pad_maximum_fusion.1
  218.7 2.4 convolution_add_fusion
  221.0 3.5 copy.327
  224.6 2.7 multiply_convert_fusion.2
  228.9 1.9 copy.329
  230.8 3.5 all-to-all-start
  234.3 16.0 %all-to-all-done = bf16[2,6,80,256]{2,0,1,3:T(2,128)(2,1)S(1)} async-done(((bf16[2,6,80,256]{2,0,1,3:T(2,128)(2,1)}), bf16[2,6,80,256]{2,0,1,3:T(2,128)(2,1)S(1)}, u32[]{:S(2)}, u32[]{:S(2)}) %all-to-all-start) | async-done | bytes 491552 | tf_op jit(solution)/shard_map/all_to_all | solution.py:171
  250.8 3.1 fusion.2
  255.3 3.5 all-to-all-start.1
  261.1 14.9 %all-to-all-done.1 = bf16[8,6,80,64]{2,3,1,0:T(8,128)(2,1)S(1)} async-done(((bf16[8,6,80,64]{2,3,1,0:T(8,128)(2,1)}), bf16[8,6,80,64]{2,3,1,0:T(8,128)(2,1)S(1)}, u32[]{:S(2)}, u32[]{:S(2)}) %all-to-all-start.1) | async-done | bytes 491552 | tf_op jit(solution)/shard_map/all_to_all | solution.py:176
  276.0 3.5 multiply_convert_fusion.1
  282.5 3.0 scatter-add.44
  285.5 4.8 dynamic-slice_add_fusion
  290.3 18.3 %scatter-add.45 = f32[2,6,18,18,256]{4,2,3,1,0:T(8,128)} dynamic-update-slice(f32[2,6,18,18,256]{4,2,3,1,0:T(8,128)} %scatter-add.44, f32[2,6,16,16,256]{4,2,3,1,0:T(8,128)} %dynamic-slice_add_fusion, s32[]{:T(128)} %constant.394.clone.1, s32[]{:T(128)} %constant.394.clone.1, s32[]{:T(128)} %bitcast.74, s32[]{:T(128)} %bitcast.75, s32[]{:T(128)} %constant.394.clone.1) | dynamic-update-slice | bytes 6291460 | tf_op jit(solution)/shard_map/scatter-add | solution.py:76
  308.5 7.0 add_select_fusion
  315.5 18.3 %scatter-add.46 = f32[2,6,18,18,256]{4,2,3,1,0:T(8,128)} dynamic-update-slice(f32[2,6,18,18,256]{4,2,3,1,0:T(8,128)} %scatter-add.45, f32[2,6,16,16,256]{4,2,3,1,0:T(8,128)} %add_select_fusion, s32[]{:T(128)} %constant.394.clone.1, s32[]{:T(128)} %constant.394.clone.1, s32[]{:T(128)} %bitcast.78, s32[]{:T(128)} %bitcast.79, s32[]{:T(128)} %constant.394.clone.1) | dynamic-update-slice | bytes 6291460 | tf_op jit(solution)/shard_map/scatter-add | solution.py:76
  333.8 5.0 slice_add_fusion.5
  338.7 17.0 %scatter-add.49 = f32[2,6,18,18,256]{4,2,3,1,0:T(8,128)} dynamic-update-slice(f32[2,6,18,18,256]{4,2,3,1,0:T(8,128)} %scatter-add.46, f32[2,6,16,16,256]{4,2,3,1,0:T(8,128)} %slice_add_fusion.5, s32[]{:T(128)} %constant.394.clone.1, s32[]{:T(128)} %constant.394.clone.1, s32[]{:T(128)} %constant.395.clone.1, s32[]{:T(128)} %constant.394.clone.1, s32[]{:T(128)} %constant.394.clone.1) | dynamic-update-slice | bytes 6291460 | tf_op jit(solution)/shard_map/scatter-add | solution.py:76
  355.7 5.0 slice_add_fusion.4
  360.6 16.9 %scatter-add.50 = f32[2,6,18,18,256]{4,2,3,1,0:T(8,128)} dynamic-update-slice(f32[2,6,18,18,256]{4,2,3,1,0:T(8,128)} %scatter-add.49, f32[2,6,16,16,256]{4,2,3,1,0:T(8,128)} %slice_add_fusion.4, s32[]{:T(128)} %constant.394.clone.1, s32[]{:T(128)} %constant.394.clone.1, s32[]{:T(128)} %constant.395.clone.1, s32[]{:T(128)} %constant.395.clone.1, s32[]{:T(128)} %constant.394.clone.1) | dynamic-update-slice | bytes 6291460 | tf_op jit(solution)/shard_map/scatter-add | solution.py:76
  377.6 5.0 slice_add_fusion.3
  382.5 16.9 %scatter-add.51 = f32[2,6,18,18,256]{4,2,3,1,0:T(8,128)} dynamic-update-slice(f32[2,6,18,18,256]{4,2,3,1,0:T(8,128)} %scatter-add.50, f32[2,6,16,16,256]{4,2,3,1,0:T(8,128)} %slice_add_fusion.3, s32[]{:T(128)} %constant.394.clone.1, s32[]{:T(128)} %constant.394.clone.1, s32[]{:T(128)} %constant.395.clone.1, s32[]{:T(128)} %constant.403.clone.1, s32[]{:T(128)} %constant.394.clone.1) | dynamic-update-slice | bytes 6291460 | tf_op jit(solution)/shard_map/scatter-add | solution.py:76
  399.5 5.0 slice_add_fusion.2
  404.4 17.0 %scatter-add.54 = f32[2,6,18,18,256]{4,2,3,1,0:T(8,128)} dynamic-update-slice(f32[2,6,18,18,256]{4,2,3,1,0:T(8,128)} %scatter-add.51, f32[2,6,16,16,256]{4,2,3,1,0:T(8,128)} %slice_add_fusion.2, s32[]{:T(128)} %constant.394.clone.1, s32[]{:T(128)} %constant.394.clone.1, s32[]{:T(128)} %constant.403.clone.1, s32[]{:T(128)} %constant.394.clone.1, s32[]{:T(128)} %constant.394.clone.1) | dynamic-update-slice | bytes 6291460 | tf_op jit(solution)/shard_map/scatter-add | solution.py:76
  421.4 5.0 slice_add_fusion.1
  426.4 16.9 %scatter-add.55 = f32[2,6,18,18,256]{4,2,3,1,0:T(8,128)} dynamic-update-slice(f32[2,6,18,18,256]{4,2,3,1,0:T(8,128)} %scatter-add.54, f32[2,6,16,16,256]{4,2,3,1,0:T(8,128)} %slice_add_fusion.1, s32[]{:T(128)} %constant.394.clone.1, s32[]{:T(128)} %constant.394.clone.1, s32[]{:T(128)} %constant.403.clone.1, s32[]{:T(128)} %constant.395.clone.1, s32[]{:T(128)} %constant.394.clone.1) | dynamic-update-slice | bytes 6291460 | tf_op jit(solution)/shard_map/scatter-add | solution.py:76
  443.3 5.0 slice_add_fusion
  448.3 16.9 %scatter-add.56 = f32[2,6,18,18,256]{4,2,3,1,0:T(8,128)} dynamic-update-slice(f32[2,6,18,18,256]{4,2,3,1,0:T(8,128)} %scatter-add.55, f32[2,6,16,16,256]{4,2,3,1,0:T(8,128)} %slice_add_fusion, s32[]{:T(128)} %constant.394.clone.1, s32[]{:T(128)} %constant.394.clone.1, s32[]{:T(128)} %constant.403.clone.1, s32[]{:T(128)} %constant.403.clone.1, s32[]{:T(128)} %constant.394.clone.1) | dynamic-update-slice | bytes 6291460 | tf_op jit(solution)/shard_map/scatter-add | solution.py:76
  465.2 2.9 convert_element_type.103
  471.1 2.8 convolution_bitcast_fusion.18
  473.9 3.1 fusion.17
  485.7 3.9 slice_convert_fusion
  489.7 13.1 %all-gather.11.cloned.1.call-done = bf16[2,48,4,16,256]{4,3,1,0,2:T(8,128)(2,1)} async-done(((bf16[2,6,4,16,256]{4,3,1,0,2:T(8,128)(2,1)}), bf16[2,48,4,16,256]{4,3,1,0,2:T(8,128)(2,1)}) %all-gather.11.cloned.1.call-update) | async-done | bytes 3145744 | tf_op jit(solution)/shard_map/all_gather | solution.py:187
  502.8 2.3 copy.345
  505.2 3.4 reshape.825
  508.6 2.6 fusion.5
  512.3 2.1 fusion.112
  514.4 5.4 scatter-add.59
  519.9 1.6 fusion.31
  521.5 1.7 slice_add_fusion.6
  523.3 5.5 scatter-add.61
  528.7 5.9 copy.351
  537.1 5.6 scatter-add.64
  542.7 3.1 multiply_convert_fusion
  556.4 76.9 %all-reduce.4.cloned.1.call-done = f32[256,80]{1,0:T(8,128)} async-done(((f32[256,80]{1,0:T(8,128)}), f32[256,80]{1,0:T(8,128)}) %all-reduce.4.cloned.1.call-update) | async-done | bytes 81936
  634.6 102.5 %reduce-scatter.5.cloned.1.call-done = f32[72,256]{1,0:T(8,128)} async-done(((f32[2304,256]{1,0:T(8,128)}), f32[72,256]{1,0:T(8,128)}) %reduce-scatter.5.cloned.1.call-update) | async-done | bytes 73744 | tf_op jit(solution)/shard_map/reduce_scatter | solution.py:183
  737.1 103.9 %reduce-scatter.3.cloned.1.call-done = f32[72,256]{1,0:T(8,128)} async-done(((f32[2304,256]{1,0:T(8,128)}), f32[72,256]{1,0:T(8,128)}) %reduce-scatter.3.cloned.1.call-update) | async-done | bytes 73744 | tf_op jit(solution)/shard_map/reduce_scatter | solution.py:196
  (193 shorter events, 69.2 us)
Async XLA Ops:
  7.2 3.7 copy-start.34
  7.2 4.5 copy-start.38
  7.2 4.8 copy-start.35
  7.2 38.7 %all-gather.5.cloned.1.call-start = ((), (), s32[]{:S(2)}) async-start(), calls=%async_computation.4 | async-start | bytes 3538944 | tf_op jit(solution)/shard_map/all_gather | solution.py:159
  10.8 95.9 %all-gather.7.cloned.1.call-start = ((), (), s32[]{:S(2)}) async-start(), calls=%async_computation.5 | async-start | bytes 2433024 | tf_op jit(solution)/shard_map/all_gather | solution.py:153
  11.6 179.8 %all-gather.9.cloned.1.call-start = ((), (), s32[]{:S(2)}) async-start(), calls=%async_computation.6 | async-start | bytes 3538944 | tf_op jit(solution)/shard_map/all_gather | solution.py:163
  54.8 2.2 copy-start.13
  60.0 55.0 %copy-start.15 = (bf16[2,6,16,16,256]{4,3,2,1,0:T(8,128)(2,1)}, bf16[2,6,16,16,256]{4,3,2,1,0:T(8,128)(2,1)S(1)}, u32[]{:S(2)}) copy-start(bf16[2,6,16,16,256]{4,3,2,1,0:T(8,128)(2,1)S(1)} %get-tuple-element.196) | copy-start | bytes 4718596
  63.6 3.7 copy-start.8
  63.6 3.7 copy-start
  106.7 2.1 copy-start.28
  108.8 1.6 copy-start.27
  110.4 1.6 copy-start.17
  115.0 1.6 copy-start.26
  116.6 1.6 copy-start.25
  118.2 1.6 copy-start.24
  121.4 1.6 copy-start.4
  123.0 1.4 copy-start.36
  204.4 9.6 %copy-start.21 = (bf16[2,6,16,16,256]{4,3,2,1,0:T(8,128)(2,1)}, bf16[2,6,16,16,256]{4,3,2,1,0:T(8,128)(2,1)S(1)}, u32[]{:S(2)}) copy-start(bf16[2,6,16,16,256]{4,3,2,1,0:T(8,128)(2,1)S(1)} %get-tuple-element.191) | copy-start | bytes 4718596
  204.4 12.5 %copy-start.19 = (bf16[2,6,16,16,256]{4,3,2,1,0:T(8,128)(2,1)}, bf16[2,6,16,16,256]{4,3,2,1,0:T(8,128)(2,1)S(1)}, u32[]{:S(2)}) copy-start(bf16[2,6,16,16,256]{4,3,2,1,0:T(8,128)(2,1)S(1)} %get-tuple-element.190) | copy-start | bytes 4718596
  208.3 1.5 copy-start.10
  208.3 2.2 copy-start.2
  210.5 1.7 copy-start.29
  214.0 1.9 copy-start.5
  227.3 1.2 copy-start.7
  228.5 5.8 copy-start.33
  230.8 19.5 %all-to-all-start = ((bf16[2,6,80,256]{2,0,1,3:T(2,128)(2,1)}), bf16[2,6,80,256]{2,0,1,3:T(2,128)(2,1)S(1)}, u32[]{:S(2)}, u32[]{:S(2)}) async-start(bf16[2,6,80,256]{2,0,1,3:T(2,128)(2,1)} %copy.329), calls=%async_computation | async-start | bytes 1572864 | tf_op jit(solution)/shard_map/all_to_all | solution.py:171
  253.9 6.4 copy-start.37
  255.3 20.7 %all-to-all-start.1 = ((bf16[8,6,80,64]{2,3,1,0:T(8,128)(2,1)}), bf16[8,6,80,64]{2,3,1,0:T(8,128)(2,1)S(1)}, u32[]{:S(2)}, u32[]{:S(2)}) async-start(bf16[8,6,80,64]{2,3,1,0:T(8,128)(2,1)} %multiply_convert_fusion.6), calls=%async_computation.1 | async-start | bytes 1572864 | tf_op jit(solution)/shard_map/all_to_all | solution.py:176
  258.8 244.0 %all-gather.11.cloned.1.call-start = ((), (), s32[]{:S(2)}) async-start(), calls=%async_computation.7 | async-start | bytes 3538944 | tf_op jit(solution)/shard_map/all_gather | solution.py:187
  276.0 3.5 copy-start.30
  276.0 3.5 copy-start.11
  465.2 3.4 copy-start.12
  468.1 1.8 copy-start.23
  470.8 162.4 %all-reduce.4.cloned.1.call-start = ((), (), s32[]{:S(2)}) async-start(), calls=%async_computation.10 | async-start | bytes 262144
  473.9 3.1 copy-start.22
  478.4 1.5 copy-start.20
  479.9 1.8 copy-start.3
  485.6 251.4 %reduce-scatter.5.cloned.1.call-start = ((), (), s32[]{:S(2)}) async-start(), calls=%async_computation.9 | async-start | bytes 2433024 | tf_op jit(solution)/shard_map/reduce_scatter | solution.py:183
  489.6 351.4 %reduce-scatter.3.cloned.1.call-start = ((), (), s32[]{:S(2)}) async-start(), calls=%async_computation.8 | async-start | bytes 2433024 | tf_op jit(solution)/shard_map/reduce_scatter | solution.py:196
  512.3 10.9 %copy-start.31 = (f32[2,6,4,16,256]{4,2,3,1,0:T(4,128)}, f32[2,6,4,16,256]{4,2,3,1,0:T(4,128)S(1)}, u32[]{:S(2)}) copy-start(f32[2,6,4,16,256]{4,2,3,1,0:T(4,128)S(1)} %fusion.29) | copy-start | bytes 2359300
  528.7 14.0 %copy-start.6 = (f32[3072,256]{1,0:T(8,128)S(1)}, f32[3072,256]{1,0:T(8,128)}, u32[]{:S(2)}) copy-start(f32[3072,256]{1,0:T(8,128)} %copy-done.4) | copy-start | bytes 9437188
  542.7 3.1 copy-start.9
  547.1 1.4 copy-start.18
  548.5 1.4 copy-start.14
  549.9 1.4 copy-start.16
  551.4 1.7 copy-start.1
  555.0 1.4 copy-start.32
Sparse Core Ops, SparseCore 0:
  11.0 34.8 all-gather.4
  49.5 57.1 all-gather.6
  124.5 31.0 all-gather.8
  471.0 31.8 all-gather.10
  508.8 124.4 all-reduce.3
  638.4 98.5 reduce-scatter.4
  742.3 98.6 reduce-scatter.2
where the time goes:
time: 861 us; the launch traced here: 850 us
  waiting for transfers between devices  396 us (46%)
  local copies, waits for them, and re-layouts  220 us (26%)
  matrix products  99.1 us (12%)
  blocking collectives  67 us (8%)
  other arithmetic  44.6 us (5%)
  between operations  15.6 us (2%)
    scatter-add x9, local copies, waits for them, and re-layouts, transpose_conv(): result.at[:, :, row_off:row_off + height, col_off:col_off + tile_w, :]  141 us
    reduce_scatter x1, waiting for transfers between devices, shards(): lax.psum_scatter(grad_one, ('face', 'member'), scatter_dimension=0, tiled...  104 us
    reduce_scatter x1, waiting for transfers between devices, shards(): lax.psum_scatter(grad_two, ('face', 'member'), scatter_dimension=0, tiled...  102 us
    unnamed x8, waiting for transfers between devices  77 us
    all_gather x1, blocking collectives, shards(): lax.all_gather(head_weight, ('face', 'member'), axis=0, tiled=True)  67 us
    dot_general x9, matrix products, transpose_conv(): lax.dot_general(flat_slope, weight[tap_index * channels:(tap_index + 1) *...  43.1 us
    all_gather x1, waiting for transfers between devices, shards(): lax.all_gather(conv_weights, ('face', 'member'), axis=0, tiled=True)  36.2 us
    all_gather x1, waiting for transfers between devices, shards(): lax.all_gather(split_edges(features), 'face', axis=1, tiled=True)  32.6 us
  transfers between devices with their start and end apart: 9, of which 8 were waited for; matrix products, arithmetic and copies ran while one was open for 11% of the time, Pallas kernels for 0%

commit v1 on v0

v1 whole, which is shorter than its diff:
```python
import functools

import jax
import jax.numpy as jnp
from jax import lax
from jax.experimental import pallas as pl
from jax.experimental.pallas import tpu as pltpu
from jax.sharding import PartitionSpec as P

smooth_sq = 0.0625
MESH = pl.DeviceIdType.MESH
VMEM = pltpu.VMEM
f32 = jnp.float32
bf16 = jnp.bfloat16
LIMIT = 60 * 1024 * 1024
NT = (((1,), (1,)), ((), ()))
TN = (((0,), (0,)), ((), ()))
NN = (((1,), (0,)), ((), ()))


def mm(a, b, dims=NN):
    return lax.dot_general(a, b, dims, preferred_element_type=f32)


def rcopy(src, dst, send, recv, **where):
    return pltpu.make_async_remote_copy(
        src_ref=src, dst_ref=dst, send_sem=send, recv_sem=recv, device_id=where, device_id_type=MESH
    )


def greet(chips, members, face_axis, member_axis):
    face = lax.axis_index("face")
    member = lax.axis_index("member")
    core = face % 2
    chip = face // 2
    barrier = pltpu.get_barrier_semaphore()
    count = 0
    if face_axis:
        pl.semaphore_signal(
            barrier, inc=1, device_id={"face": chip * 2 + 1 - core}, device_id_type=MESH
        )
        for j in range(1, chips):
            pl.semaphore_signal(
                barrier,
                inc=1,
                device_id={"face": ((chip + j) % chips) * 2 + core},
                device_id_type=MESH,
            )
        count += chips
    if member_axis:
        for j in range(1, members):
            pl.semaphore_signal(
                barrier, inc=1, device_id={"member": (member + j) % members}, device_id_type=MESH
            )
        count += members - 1
    pl.semaphore_wait(barrier, count)


def line_gather(x_ref, out_at, member, members, sems):
    ups, upr, dns, dnr = sems
    steps = members - 1

    def up(s):
        b = jnp.maximum(member - s, 0)
        return rcopy(
            x_ref if s == 0 else out_at(b),
            out_at(b),
            ups.at[s],
            upr.at[s],
            member=jnp.minimum(member + 1, members - 1),
        )

    def down(s):
        b = jnp.minimum(member + s, members - 1)
        return rcopy(
            x_ref if s == 0 else out_at(b),
            out_at(b),
            dns.at[s],
            dnr.at[s],
            member=jnp.maximum(member - 1, 0),
        )

    def up_goes(s):
        return jnp.logical_and(member - s >= 0, member < members - 1)

    def down_goes(s):
        return jnp.logical_and(member + s < members, member > 0)

    pl.when(up_goes(0))(lambda: up(0).start())
    pl.when(down_goes(0))(lambda: down(0).start())
    for s in range(steps):
        pl.when(member - 1 - s >= 0)(lambda: up(s).wait_recv())
        if s + 1 < steps:
            pl.when(up_goes(s + 1))(lambda: up(s + 1).start())
        pl.when(member + 1 + s < members)(lambda: down(s).wait_recv())
        if s + 1 < steps:
            pl.when(down_goes(s + 1))(lambda: down(s + 1).start())
    for s in range(steps):
        pl.when(up_goes(s))(lambda: up(s).wait_send())
        pl.when(down_goes(s))(lambda: down(s).wait_send())


class FaceGather:
    def __init__(self, src, out, chips, sems):
        self.src, self.out, self.chips = src, out, chips
        self.send, self.recv, self.fsend, self.frecv = sems
        face = lax.axis_index("face")
        self.face, self.core, self.chip = face, face % 2, face // 2
        self.partner = self.chip * 2 + 1 - self.core

    def direct(self, j):
        return rcopy(
            self.src,
            self.out.at[self.face],
            self.send.at[j],
            self.recv.at[j],
            face=((self.chip + j) % self.chips) * 2 + self.core,
        )

    def forward(self, j):
        block = ((self.chip + self.chips - j) % self.chips) * 2 + self.core
        return rcopy(
            self.src if j == 0 else self.out.at[block],
            self.out.at[block],
            self.fsend.at[j],
            self.frecv.at[j],
            face=self.partner,
        )

    def start(self):
        for j in range(1, self.chips):
            self.direct(j).start()
        self.forward(0).start()

    def relay(self):
        for j in range(1, self.chips):
            self.direct(j).wait_recv()
            self.forward(j).start()

    def finish(self):
        for j in range(1, self.chips):
            self.direct(j).wait_send()
        for j in range(self.chips):
            self.forward(j).wait()


def dma_sems(*sizes):
    return [pltpu.SemaphoreType.DMA((max(n, 1),)) for n in sizes]


def first_gather_kernel(chips, members, count, *refs):
    edges, ws = refs[0], refs[1 : 1 + count]
    edges_out, outs = refs[1 + count], refs[2 + count : 2 + 2 * count]
    sems = refs[2 + 2 * count :]
    own_sem, sems = sems[0], sems[1:]
    face = lax.axis_index("face")
    member = lax.axis_index("member")
    own = [pltpu.make_async_copy(edges, edges_out.at[face], own_sem.at[0])]
    for k in range(count):
        own.append(
            pltpu.make_async_copy(ws[k], outs[k].at[face, member], own_sem.at[k + 1])
        )
    for c in own:
        c.start()
    greet(chips, members, True, True)
    eg = FaceGather(edges, edges_out, chips, sems[:4])
    eg.start()
    for c in own:
        c.wait()
    rest = sems[4:]
    wgs = []
    for k in range(count):
        line = rest[8 * k : 8 * k + 4]
        line_gather(ws[k], lambda b: outs[k].at[face, b], member, members, line)
        wg = FaceGather(outs[k].at[face], outs[k], chips, rest[8 * k + 4 : 8 * k + 8])
        wg.start()
        wgs.append(wg)
    eg.relay()
    for wg in wgs:
        wg.relay()
    eg.finish()
    for wg in wgs:
        wg.finish()


def first_gather(edges, ws, faces, members):
    chips = faces // 2
    count = len(ws)
    shapes = [jax.ShapeDtypeStruct((faces,) + edges.shape, edges.dtype)] + [
        jax.ShapeDtypeStruct((faces, members) + w.shape, w.dtype) for w in ws
    ]
    sems = dma_sems(count + 1) + dma_sems(*([chips] * 4))
    for _ in ws:
        sems += dma_sems(*([members] * 4)) + dma_sems(*([chips] * 4))
    return pl.pallas_call(
        functools.partial(first_gather_kernel, chips, members, count),
        out_shape=shapes,
        in_specs=[pl.BlockSpec(memory_space=VMEM)] * (count + 1),
        out_specs=[pl.BlockSpec(memory_space=VMEM)] * (count + 1),
        scratch_shapes=sems,
        compiler_params=pltpu.CompilerParams(
            collective_id=1, has_side_effects=True, vmem_limit_bytes=LIMIT
        ),
        name="first_gather",
    )(edges, *ws)


def face_gather_kernel(chips, x, out, own_sem, *sems):
    own = pltpu.make_async_copy(x, out.at[lax.axis_index("face")], own_sem.at[0])
    own.start()
    greet(chips, 1, True, False)
    g = FaceGather(x, out, chips, sems)
    g.start()
    own.wait()
    g.relay()
    g.finish()


def face_gather(x, faces, ident):
    chips = faces // 2
    return pl.pallas_call(
        functools.partial(face_gather_kernel, chips),
        out_shape=jax.ShapeDtypeStruct((faces,) + x.shape, x.dtype),
        in_specs=[pl.BlockSpec(memory_space=VMEM)],
        out_specs=pl.BlockSpec(memory_space=VMEM),
        scratch_shapes=dma_sems(1) + dma_sems(*([chips] * 4)),
        compiler_params=pltpu.CompilerParams(
            collective_id=ident, has_side_effects=True, vmem_limit_bytes=LIMIT
        ),
        name="face_gather",
    )(x)


def member_gather_kernel(members, x, out, own_sem, *sems):
    member = lax.axis_index("member")
    own = pltpu.make_async_copy(x, out.at[member], own_sem.at[0])
    own.start()
    greet(1, members, False, True)
    line_gather(x, lambda b: out.at[b], member, members, sems)
    own.wait()


def member_gather(x, members, ident):
    return pl.pallas_call(
        functools.partial(member_gather_kernel, members),
        out_shape=jax.ShapeDtypeStruct((members,) + x.shape, x.dtype),
        in_specs=[pl.BlockSpec(memory_space=VMEM)],
        out_specs=pl.BlockSpec(memory_space=VMEM),
        scratch_shapes=dma_sems(1) + dma_sems(*([members] * 4)),
        compiler_params=pltpu.CompilerParams(
            collective_id=ident, has_side_effects=True, vmem_limit_bytes=LIMIT
        ),
        name="member_gather",
    )(x)


def scatter_kernel(chips, members, count, *refs):
    gs, outs = refs[:count], refs[count : 2 * count]
    scratch = refs[2 * count :]
    face = lax.axis_index("face")
    member = lax.axis_index("member")
    core, chip = face % 2, face // 2
    partner = chip * 2 + 1 - core
    greet(chips, members, True, True)

    def parts(k):
        return scratch[10 * k : 10 * k + 10]

    def there(j):
        return (chip + j) % chips

    def core_copy(k, j):
        fromcore, _, _, _, s0, r0, _, _, _, _ = parts(k)
        return rcopy(
            gs[k].at[there(j), 1 - core], fromcore.at[j], s0.at[j], r0.at[j], face=partner
        )

    def chip_copy(k, j):
        _, acc, fromchip, _, _, _, s1, r1, _, _ = parts(k)
        return rcopy(acc.at[j], fromchip.at[j], s1.at[j], r1.at[j], face=there(j) * 2 + core)

    def line_copy(k, j):
        _, acc, _, fromline, _, _, _, _, s2, r2 = parts(k)
        to = (member + j) % members
        return rcopy(acc.at[0, to], fromline.at[j], s2.at[j], r2.at[j], member=to)

    order = list(range(1, chips)) + [0]
    for k in range(count):
        for j in order:
            core_copy(k, j).start()
    for k in range(count):
        fromcore, acc = parts(k)[:2]
        for j in order:
            core_copy(k, j).wait_recv()
            acc[j] = gs[k][there(j), core] + fromcore[j]
            if j:
                chip_copy(k, j).start()
    for k in range(count):
        acc, fromchip = parts(k)[1:3]
        for j in range(1, chips):
            chip_copy(k, j).wait_recv()
            acc[0] = acc[0] + fromchip[j]
        for j in range(1, members):
            line_copy(k, j).start()
    for k in range(count):
        acc, fromline = parts(k)[1], parts(k)[3]
        total = acc[0, member]
        for j in range(1, members):
            line_copy(k, j).wait_recv()
            total = total + fromline[j]
        outs[k][...] = total
    for k in range(count):
        for j in range(chips):
            core_copy(k, j).wait_send()
        for j in range(1, chips):
            chip_copy(k, j).wait_send()
        for j in range(1, members):
            line_copy(k, j).wait_send()


def scatter(gs, faces, members, ident):
    chips = faces // 2
    scratch = []
    for g in gs:
        tail = g.shape[3:]
        scratch += [
            VMEM((chips, members) + tail, f32),
            VMEM((chips, members) + tail, f32),
            VMEM((chips, members) + tail, f32),
            VMEM((members,) + tail, f32),
        ] + dma_sems(chips, chips, chips, chips, members, members)
    return pl.pallas_call(
        functools.partial(scatter_kernel, chips, members, len(gs)),
        out_shape=[jax.ShapeDtypeStruct(g.shape[3:], f32) for g in gs],
        in_specs=[pl.BlockSpec(memory_space=VMEM)] * len(gs),
        out_specs=[pl.BlockSpec(memory_space=VMEM)] * len(gs),
        scratch_shapes=scratch,
        compiler_params=pltpu.CompilerParams(
            collective_id=ident, has_side_effects=True, vmem_limit_bytes=LIMIT
        ),
        name="scatter",
    )(*gs)


def rims_of(index_ref, flip_ref, edges_ref, n, length):
    cat = jnp.concatenate([edges_ref[index_ref[n * 4 + a]] for a in range(4)], axis=0)
    size = 4 * length
    row = lax.broadcasted_iota(jnp.int32, (size, size), 0)
    col = lax.broadcasted_iota(jnp.int32, (size, size), 1)
    side = row // length
    place = row - side * length
    flag = jnp.zeros((size, size), jnp.int32)
    for a in range(4):
        flag = jnp.where(side == a, flip_ref[n * 4 + a], flag)
    target = side * length + jnp.where(flag == 1, length - 1 - place, place)
    return mm(jnp.where(col == target, 1.0, 0.0).astype(bf16), cat)


def col_to_rows(ref_slice):
    height, _, channels = ref_slice.shape
    return ref_slice.reshape(height, channels)


def sides_out(field, edge_ref, k):
    w = field.shape[1]
    h = field.shape[0]
    edge_ref[k, 0] = field[0].astype(bf16)
    edge_ref[k, 1] = col_to_rows(field[:, w - 1 : w, :]).astype(bf16)
    edge_ref[k, 2] = field[h - 1].astype(bf16)
    edge_ref[k, 3] = col_to_rows(field[:, 0:1, :]).astype(bf16)


def silu(v):
    return v / (1.0 + jnp.exp(-v))


def dsilu(v):
    s = 1.0 / (1.0 + jnp.exp(-v))
    return s * (1.0 + v * (1.0 - s))


def conv_kernel(block, last, *refs):
    index_ref, flip_ref, x_ref, edges_ref, w_ref = refs[:5]
    if last:
        head_ref, x3_ref, pre_ref, act_ref, out_ref, pad = refs[5:]
    else:
        x3_ref, pre_ref, act_ref, side_ref, pad, field = refs[5:]
    _, h, w, c = x_ref.shape
    step = pl.program_id(0)
    for k in range(block):
        n = step * block + k
        rims = rims_of(index_ref, flip_ref, edges_ref, n, w)
        zero = jnp.zeros((8, c), f32)
        for r in (0, h + 1):
            pad[r, 0:8, :] = zero
            pad[r, 8 + w : 16 + w, :] = zero
        pad[1 : h + 1, 8 : 8 + w, :] = x_ref[k].astype(f32)
        pad[0, 8 : 8 + w, :] = rims[0:w]
        pad[1 : h + 1, 8 + w : 9 + w, :] = rims[w : w + h].reshape(h, 1, c)
        pad[h + 1, 8 : 8 + w, :] = rims[w + h : 2 * w + h]
        pad[1 : h + 1, 7:8, :] = rims[2 * w + h :].reshape(h, 1, c)
        for b in range(3):
            x3_ref[k, :, :, b * c : (b + 1) * c] = pad[:, 7 + b : 7 + b + w, :].astype(bf16)
    pre = None
    for a in range(3):
        part = mm(
            x3_ref[:, a : a + h].reshape(block * h * w, 3 * c),
            w_ref[3 * a * c : 3 * (a + 1) * c, :],
        )
        pre = part if pre is None else pre + part
    pre_ref[...] = pre.reshape(block, h * w, c)
    act = silu(pre).astype(bf16)
    act_ref[...] = act.reshape(act_ref.shape)
    if last:
        for k in range(block):
            out_ref[k] = mm(head_ref[...], act[k * h * w : (k + 1) * h * w], NT).astype(bf16)
    else:
        for k in range(block):
            field[...] = act[k * h * w : (k + 1) * h * w].astype(f32).reshape(h, w, c)
            sides_out(field, side_ref, k)


def whole(shape):
    return pl.BlockSpec(shape, lambda i: (0,) * len(shape))


def tiles(block, shape):
    return pl.BlockSpec((block,) + shape, lambda i: (i,) + (0,) * len(shape))


SMEM_SPEC = pl.BlockSpec(memory_space=pltpu.SMEM)


def block_of(n):
    return 3 if n % 3 == 0 else (2 if n % 2 == 0 else 1)


def conv(index, flips, x, edges, w, head_t=None):
    n, h, wd, c = x.shape
    block = block_of(n)
    last = head_t is not None
    in_specs = [
        SMEM_SPEC,
        SMEM_SPEC,
        tiles(block, (h, wd, c)),
        whole(edges.shape),
        whole(w.shape),
    ]
    shapes = [
        jax.ShapeDtypeStruct((n, h + 2, wd, 3 * c), bf16),
        jax.ShapeDtypeStruct((n, h * wd, c), f32),
        jax.ShapeDtypeStruct((n, h * wd, c) if last else (n, h, wd, c), bf16),
    ]
    args = [index, flips, x, edges, w]
    scratch = [VMEM((h + 2, wd + 16, c), f32)]
    if last:
        in_specs.append(whole(head_t.shape))
        args.append(head_t)
        shapes.append(jax.ShapeDtypeStruct((n, head_t.shape[0], h * wd), bf16))
    else:
        shapes.append(jax.ShapeDtypeStruct((n, 4, wd, c), bf16))
        scratch.append(VMEM((h, wd, c), f32))
    return pl.pallas_call(
        functools.partial(conv_kernel, block, last),
        grid=(n // block,),
        out_shape=shapes,
        in_specs=in_specs,
        out_specs=[tiles(block, s.shape[1:]) for s in shapes],
        scratch_shapes=scratch,
        compiler_params=pltpu.CompilerParams(vmem_limit_bytes=LIMIT),
        name="conv_last" if last else "conv_first",
    )(*args)


def back_kernel(block, ensemble, tile_dev, h, w, *refs):
    y_ref, own_ref, obs_ref, act_ref, pre_ref, head_ref, w_ref = refs[:7]
    slope_ref, inner_ref, side_ref, hg_ref, va, vb, pad, s3, cols = refs[7:]
    c = act_ref.shape[-1]
    step = pl.program_id(0)

    @pl.when(step == 0)
    def _():
        hg_ref[...] = jnp.zeros_like(hg_ref)
        for a in range(3):
            for b in range(3):
                tap = w_ref[(3 * a + b) * c : (3 * a + b + 1) * c, :]
                va[a, :, b * c : (b + 1) * c] = tap
                if b == 0:
                    vb[0, :, a * c : (a + 1) * c] = tap
                if b == 2:
                    vb[1, :, a * c : (a + 1) * c] = tap
        pad[...] = jnp.zeros_like(pad)

    for k in range(block):
        t = (step * block + k) % tile_dev
        y = own_ref[k].astype(f32)

        def g(x):
            return x * lax.rsqrt(x * x + smooth_sq)

        gap = g(y - obs_ref[t].astype(f32))
        paired = jnp.zeros_like(y)
        for m in range(ensemble):
            paired = paired + g(y - y_ref[m, t].astype(f32))
        slope_out = ((gap / ensemble - paired / (ensemble * ensemble)) / h).astype(bf16)
        hg_ref[...] += mm(slope_out, act_ref[k])
        back = mm(slope_out, head_ref[...], TN)
        slope = (back * dsilu(pre_ref[k])).astype(bf16)
        slope_ref[k] = slope
        pad[2 : h + 2, 8 : 8 + w, :] = slope.astype(f32).reshape(h, w, c)
        for b in range(3):
            s3[k, :, :, b * c : (b + 1) * c] = pad[:, 9 - b : 9 - b + w, :].astype(bf16)
        left = pad[:, 8:9, :].reshape(h + 4, c)
        right = pad[:, 7 + w : 8 + w, :].reshape(h + 4, c)
        for a in range(3):
            cols[0, k, :, a * c : (a + 1) * c] = left[3 - a : 3 - a + h].astype(bf16)
            cols[1, k, :, a * c : (a + 1) * c] = right[3 - a : 3 - a + h].astype(bf16)
    full = None
    for a in range(3):
        part = mm(s3[:, 2 - a : 20 - a + h - 16].reshape(block * (h + 2) * w, 3 * c), va[a], NT)
        full = part if full is None else full + part
    full = full.reshape(block, h + 2, w, c).astype(bf16)
    inner_ref[...] = full[:, 1 : h + 1]
    lefts = mm(cols[0].reshape(block * h, 3 * c), vb[0], NT).astype(bf16)
    rights = mm(cols[1].reshape(block * h, 3 * c), vb[1], NT).astype(bf16)
    for k in range(block):
        side_ref[k, 0] = full[k, 0]
        side_ref[k, 1] = rights[k * h : (k + 1) * h]
        side_ref[k, 2] = full[k, h + 1]
        side_ref[k, 3] = lefts[k * h : (k + 1) * h]


def backward(y_all, own, obs, act, pre, head_t, w, h, wd):
    n, cells, c = act.shape
    ensemble, tile_dev = y_all.shape[:2]
    block = block_of(n)
    shapes = [
        jax.ShapeDtypeStruct((n, cells, c), bf16),
        jax.ShapeDtypeStruct((n, h, wd, c), bf16),
        jax.ShapeDtypeStruct((n, 4, wd, c), bf16),
        jax.ShapeDtypeStruct(head_t.shape, f32),
    ]
    return pl.pallas_call(
        functools.partial(back_kernel, block, ensemble, tile_dev, h, wd),
        grid=(n // block,),
        out_shape=shapes,
        in_specs=[
            whole(y_all.shape),
            tiles(block, own.shape[1:]),
            whole(obs.shape),
            tiles(block, (cells, c)),
            tiles(block, (cells, c)),
            whole(head_t.shape),
            whole(w.shape),
        ],
        out_specs=[tiles(block, s.shape[1:]) for s in shapes[:3]] + [whole(head_t.shape)],
        scratch_shapes=[
            VMEM((3, c, 3 * c), bf16),
            VMEM((2, c, 3 * c), bf16),
            VMEM((h + 4, wd + 16, c), f32),
            VMEM((block, h + 4, wd, 3 * c), bf16),
            VMEM((2, block, h, 3 * c), bf16),
        ],
        compiler_params=pltpu.CompilerParams(vmem_limit_bytes=LIMIT),
        name="backward",
    )(y_all, own, obs, act, pre, head_t, w)


def grad_kernel(block, steps, mid, h, w, *refs):
    if mid:
        index_ref, flip_ref, edges_ref, inner_ref, pre_ref, x3_ref, out_ref, acc, field = refs
    else:
        slope_ref, x3_ref, out_ref, acc = refs
    c = out_ref.shape[-1]
    step = pl.program_id(0)

    @pl.when(step == 0)
    def _():
        acc[...] = jnp.zeros_like(acc)

    slopes = []
    for k in range(block):
        if mid:
            rims = rims_of(index_ref, flip_ref, edges_ref, step * block + k, w)
            field[...] = inner_ref[k].astype(f32)
            field[0] += rims[0:w]
            field[:, w - 1 : w, :] += rims[w : w + h].reshape(h, 1, c)
            field[h - 1] += rims[w + h : 2 * w + h]
            field[:, 0:1, :] += rims[2 * w + h :].reshape(h, 1, c)
            slope = (field[...].reshape(h * w, c) * dsilu(pre_ref[k])).astype(bf16)
        else:
            slope = slope_ref[k]
        slopes.append(slope.T)
    turned = jnp.concatenate(slopes, axis=1)
    for a in range(3):
        acc[a] += mm(turned, x3_ref[:, a : a + h].reshape(block * h * w, 3 * c))

    @pl.when(step == steps - 1)
    def _():
        for a in range(3):
            for b in range(3):
                out_ref[(3 * a + b) * c : (3 * a + b + 1) * c, :] = acc[
                    a, :, b * c : (b + 1) * c
                ].T


def weight_grad(x3, h, w, c, slope=None, mid=None):
    n = x3.shape[0]
    block = block_of(n)
    steps = n // block
    scratch = [VMEM((3, c, 3 * c), f32)]
    if mid is None:
        args = [slope, x3]
        in_specs = [tiles(block, slope.shape[1:]), tiles(block, x3.shape[1:])]
    else:
        index, flips, edges, inner, pre = mid
        args = [index, flips, edges, inner, pre, x3]
        in_specs = [
            SMEM_SPEC,
            SMEM_SPEC,
            whole(edges.shape),
            tiles(block, inner.shape[1:]),
            tiles(block, pre.shape[1:]),
            tiles(block, x3.shape[1:]),
        ]
        scratch.append(VMEM((h, w, c), f32))
    return pl.pallas_call(
        functools.partial(grad_kernel, block, steps, mid is not None, h, w),
        grid=(steps,),
        out_shape=jax.ShapeDtypeStruct((9 * c, c), f32),
        in_specs=in_specs,
        out_specs=whole((9 * c, c)),
        scratch_shapes=scratch,
        compiler_params=pltpu.CompilerParams(vmem_limit_bytes=LIMIT),
        name="grad_two" if mid is None else "grad_one",
    )(*args)


def split_edges(x):
    return jnp.stack([x[:, 0], x[:, :, -1], x[:, -1], x[:, :, 0]], axis=1)


def edge_table(adjacency, placement_map, first_slot, members, tile_dev):
    total = placement_map.shape[0]
    ids = jnp.arange(total, dtype=jnp.int32)
    mine = first_slot + jnp.arange(tile_dev, dtype=jnp.int32)
    my_tiles = jnp.sum(jnp.where(ids[None] == mine[:, None], placement_map[None], 0), axis=1)
    hit = ids[None, :] == my_tiles[:, None]
    entries = jnp.sum(jnp.where(hit[:, :, None, None], adjacency[None], 0), axis=1)
    neighbour, side, flip = entries[:, :, 0], entries[:, :, 1], entries[:, :, 2]
    found = neighbour[:, :, None] == placement_map[None, None, :]
    slot = jnp.sum(jnp.where(found, ids[None, None, :], 0), axis=2)
    face, inner = slot // tile_dev, slot % tile_dev
    m = jnp.arange(members, dtype=jnp.int32)[:, None, None]
    index = ((face[None] * members + m) * tile_dev + inner[None]) * 4 + side[None]
    flips = jnp.broadcast_to(flip[None], index.shape)
    return index.reshape(-1), flips.reshape(-1)


def shards(faces, zs, features, observed, conv_weights, head_weight, adjacency, placement_map):
    members, tile_dev, h, w, c = features.shape
    n = members * tile_dev
    variables = head_weight.shape[1]
    index, flips = edge_table(
        adjacency, placement_map, lax.axis_index("face") * tile_dev, members, tile_dev
    )
    x = features.reshape(n, h, w, c)
    rows = conv_weights.shape[0]
    head_rows = head_weight.shape[0]
    lanes = -(-variables // 128) * 128
    head_wide = jnp.pad(head_weight, ((0, 0), (0, lanes - variables)))
    edges, w0, w1, head = first_gather(
        split_edges(x), [conv_weights[:, 0], conv_weights[:, 1], head_wide], faces, zs
    )
    w0 = w0.reshape(faces * zs * rows, c)
    w1 = w1.reshape(faces * zs * rows, c)
    head_t = head.reshape(faces * zs * head_rows, lanes)[:, :variables].T
    obs = lax.all_gather(observed, "member", axis=2, tiled=True)

    def flat(e):
        return e.reshape((faces * n * 4,) + e.shape[-2:])

    x3_one, pre_one, act_one, sides = conv(index, flips, x, flat(edges), w0)
    x3_two, pre_two, act_two, outs = conv(
        index, flips, act_one, flat(face_gather(sides, faces, 2)), w1, head_t
    )
    y_all = member_gather(outs, zs, 3).reshape(zs * members, tile_dev, variables, h * w)
    slope_two, inner, borders, hg = backward(
        y_all, outs, obs, act_two, pre_two, head_t, w1, h, w
    )
    grad_two = weight_grad(x3_two, h, w, c, slope=slope_two)
    returned = flat(face_gather(borders, faces, 4))
    grad_one = weight_grad(x3_one, h, w, c, mid=(index, flips, returned, inner, pre_one))
    hg = jnp.pad(hg.T, ((0, 0), (0, lanes - variables)))
    chips = faces // 2
    one, two, head_out = scatter(
        [
            grad_one.reshape(chips, 2, zs, rows, c),
            grad_two.reshape(chips, 2, zs, rows, c),
            hg.reshape(chips, 2, zs, head_rows, lanes),
        ],
        faces,
        zs,
        5,
    )
    return jnp.stack([one, two], axis=1), head_out[:, :variables]


def solution(mesh):
    in_specs = (
        P("member", "face", None, None, None),
        P("face", None, "member"),
        P(("face", "member"), None, None),
        P(("face", "member"), None),
        P(),
        P(),
    )
    out_specs = (P(("face", "member"), None, None), P(("face", "member"), None))
    body = functools.partial(shards, mesh.shape["face"], mesh.shape["member"])
    return jax.shard_map(body, mesh=mesh, in_specs=in_specs, out_specs=out_specs, check_vma=False)
```

time: 861 us -> 262 us (0.30); the launches traced: 850 us -> 261 us
  waiting for transfers between devices: 396 us -> 0 us
  Pallas kernels: 0 us -> 226 us
  local copies, waits for them, and re-layouts: 220 us -> 12.7 us
  matrix products: 99.1 us -> 0 us
  blocking collectives: 67 us -> 16.5 us
  other arithmetic: 44.6 us -> 4.66 us
  between operations: 15.6 us -> 0.76 us
    pallas_call x0 -> x10, Pallas kernels: none -> 226 us  [the longest x2 48.9 us: face_gather(): pl.pallas_call(functools.partial(face_gather_kernel, chips), out_shape=ja...]
    reduce_scatter x2 -> x0, waiting for transfers between devices: 206 us -> none  [the longest x1 104 us: shards(): lax.psum_scatter(grad_one, ('face', 'member'), scatter_dimension=0, tiled...]
    scatter-add x13 -> x0, local copies, waits for them, and re-layouts: 164 us -> none  [the longest x9 141 us: transpose_conv(): result.at[:, :, row_off:row_off + height, col_off:col_off + tile_w, :]]
    dot_general x51 -> x0, matrix products: 99.1 us -> none  [the longest x9 43.1 us: transpose_conv(): lax.dot_general(flat_slope, weight[tap_index * channels:(tap_index + 1) *...]
    all_gather x4 -> x0, waiting for transfers between devices: 82 us -> none  [the longest x1 36.2 us: shards(): lax.all_gather(conv_weights, ('face', 'member'), axis=0, tiled=True)]
    unnamed x8 -> x0, waiting for transfers between devices: 77 us -> none
    all_gather x1, blocking collectives: 67 us -> 16.5 us  [shards(): obs = lax.all_gather(observed, 'member', axis=2, tiled=True)]
    all_to_all x2 -> x0, waiting for transfers between devices: 30.9 us -> none  [the longest x1 16 us: shards(): lax.all_to_all(outputs, 'member', split_axis=3, concat_axis=0, tiled=True)]
  transfers between devices with their start and end apart: 9 -> 0, of which waited for: 8 -> 0; matrix products, arithmetic and copies ran while one was open for 11% -> 0% of each run, Pallas kernels for 0% -> 0%
where the time goes in v1:
time: 262 us; the launch traced here: 261 us
  Pallas kernels  226 us (86%)
  blocking collectives  16.5 us (6%)
  local copies, waits for them, and re-layouts  12.7 us (5%)
  other arithmetic  4.66 us (2%)
    pallas_call x2, Pallas kernels, face_gather(): pl.pallas_call(functools.partial(face_gather_kernel, chips), out_shape=ja...  48.9 us
    pallas_call x1, Pallas kernels, scatter(): pl.pallas_call(functools.partial(scatter_kernel, chips, members, len(gs))...  43.6 us
    pallas_call x1, Pallas kernels, member_gather(): pl.pallas_call(functools.partial(member_gather_kernel, members), out_shap...  42.2 us
    pallas_call x1, Pallas kernels, first_gather(): pl.pallas_call(functools.partial(first_gather_kernel, chips, members, cou...  39.3 us
    pallas_call x2, Pallas kernels, weight_grad(): pl.pallas_call(functools.partial(grad_kernel, block, steps, mid is not No...  20 us
    pallas_call x2, Pallas kernels, conv(): pl.pallas_call(functools.partial(conv_kernel, block, last), grid=(n // bl...  19.4 us
    all_gather x1, blocking collectives, shards(): obs = lax.all_gather(observed, 'member', axis=2, tiled=True)  16.5 us
    pallas_call x1, Pallas kernels, backward(): pl.pallas_call(functools.partial(back_kernel, block, ensemble, tile_dev,...  13.1 us

profile of v1, /device:TPU:0, one launch (start us, length us, event | category | flops | bytes accessed | tf_op | source)
XLA Modules:
  0.0 261.0 jit_solution(5984988816723882996)
XLA Ops:
  0.6 0.8 select_reduce_fusion.2
  1.5 0.1 iota_compare_fusion.1
  1.6 1.3 pad.8.refs_3_
  2.8 1.1 select_reduce_fusion
  3.9 0.1 copy.50
  4.0 0.1 copy.51
  4.1 0.1 copy.48
  4.2 0.1 copy.49
  4.3 0.1 copy.46
  4.4 0.1 copy.47
  4.5 0.9 select_reduce_fusion.1
  5.4 0.6 reshape.99.refs_1_
  6.0 0.6 reshape.111.refs_0_
  6.6 1.1 fusion.4
  7.7 0.6 copy_bitcast_fusion.2
  8.3 1.0 fusion.2
  9.3 16.5 %all_gather.3 = bf16[6,80,256]{1,2,0:T(8,128)(2,1)S(1)} all-gather(bf16[6,80,64]{1,2,0:T(8,128)(2,1)} %param.7), channel_id=1, replica_groups=mesh['face'=8,'member'=4] {'member'}, dimensions={2}, use_global_device_ids=true | all-gather | bytes 307200 | tf_op jit(solution)/shard_map/all_gather | solution.py:678
  25.8 0.9 copy.57.refs_2_
  26.7 1.8 fusion.3
  28.5 0.8 pad_maximum_fusion.refs_0_
  29.3 39.3 %first_gather.1 = (bf16[8,12,4,16,256]{4,3,2,1,0:T(8,128)(2,1)}, bf16[8,4,72,256]{3,2,1,0:T(8,128)(2,1)}, bf16[8,4,72,256]{3,2,1,0:T(8,128)(2,1)}, bf16[8,4,8,128]{3,2,1,0:T(8,128)(2,1)}) custom-call(bf16[12,4,16,256]{3,2,1,0:T(8,128)(2,1)} %pad_maximum_fusion.refs_0_, bf16[72,256]{1,0:T(8,128)(2,1)} %get-tuple-element.60.refs_1_, ...), custom_call_target="tpu_custom_call" | custom-call | tf_op jit(solution)/shard_map/first_gather/pallas_call | solution.py:195
  68.6 1.5 copy.64
  70.1 9.8 %conv_first.1 = (bf16[12,18,16,768]{3,2,1,0:T(8,128)(2,1)}, f32[12,256,256]{2,1,0:T(8,128)}, bf16[12,16,16,256]{3,2,1,0:T(8,128)(2,1)}, bf16[12,4,16,256]{3,2,1,0:T(8,128)(2,1)}) custom-call(s32[48]{0:T(128)} %reshape.111.refs_0_, s32[48]{0:T(128)} %reshape.99.refs_1_, bf16[12,16,16,256]{3,2,1,0:T(8,128)(2,1)} %bitcast.42, bf16[384,16,256]{2,1,0:T(8,128)(2,1)} %bitcast.39, ...), custom_call_target="tpu_custom_call" | custom-call | tf_op jit(solution)/shard_map/conv_first/pallas_call | solution.py:463
  79.9 24.8 %face_gather.2 = bf16[8,12,4,16,256]{4,3,2,1,0:T(8,128)(2,1)} custom-call(bf16[12,4,16,256]{3,2,1,0:T(8,128)(2,1)} %get-tuple-element.24.x), custom_call_target="tpu_custom_call" | custom-call | tf_op jit(solution)/shard_map/face_gather/pallas_call | solution.py:221
  104.7 9.6 %conv_last.1 = (bf16[12,18,16,768]{3,2,1,0:T(8,128)(2,1)}, f32[12,256,256]{2,1,0:T(8,128)}, bf16[12,256,256]{2,1,0:T(8,128)(2,1)}, bf16[12,80,256]{2,1,0:T(8,128)(2,1)}) custom-call(s32[48]{0:T(128)} %reshape.111.refs_0_, s32[48]{0:T(128)} %reshape.99.refs_1_, bf16[12,16,16,256]{3,2,1,0:T(8,128)(2,1)} %get-tuple-element.23.refs_2_, ...), custom_call_target="tpu_custom_call" | custom-call | tf_op jit(solution)/shard_map/conv_last/pallas_call | solution.py:463
  114.3 42.2 %member_gather.1 = bf16[4,12,80,256]{3,2,1,0:T(8,128)(2,1)} custom-call(bf16[12,80,256]{2,1,0:T(8,128)(2,1)} %get-tuple-element.27.x.refs_1_), custom_call_target="tpu_custom_call" | custom-call | tf_op jit(solution)/shard_map/member_gather/pallas_call | solution.py:244
  156.5 13.1 %backward.1 = (bf16[12,256,256]{2,1,0:T(8,128)(2,1)}, bf16[12,16,16,256]{3,2,1,0:T(8,128)(2,1)}, bf16[12,4,16,256]{3,2,1,0:T(8,128)(2,1)}, f32[80,256]{1,0:T(8,128)}) custom-call(bf16[8,6,80,256]{3,2,1,0:T(8,128)(2,1)} %bitcast.36, bf16[12,80,256]{2,1,0:T(8,128)(2,1)} %get-tuple-element.27.x.refs_1_, bf16[6,80,256]{2,1,0:T(8,128)(2,1)} %copy.57.refs_2_, ...), custom_call_target="tpu_custom_call" | custom-call | tf_op jit(solution)/shard_map/backward/pallas_call | solution.py:543
  169.5 0.0 copy-start
  169.5 8.6 %grad_two.1 = f32[2304,256]{1,0:T(8,128)} custom-call(bf16[12,256,256]{2,1,0:T(8,128)(2,1)} %get-tuple-element.34.refs_0_, bf16[12,18,16,768]{3,2,1,0:T(8,128)(2,1)} %get-tuple-element.35.refs_1_), custom_call_target="tpu_custom_call" | custom-call | tf_op jit(solution)/shard_map/grad_two/pallas_call | solution.py:627
  178.2 0.0 copy-done
  178.2 0.1 copy.65
  178.3 0.7 pad.9.clone
  179.0 24.1 %face_gather.3 = bf16[8,12,4,16,256]{4,3,2,1,0:T(8,128)(2,1)} custom-call(bf16[12,4,16,256]{3,2,1,0:T(8,128)(2,1)} %get-tuple-element.30.x), custom_call_target="tpu_custom_call" | custom-call | tf_op jit(solution)/shard_map/face_gather/pallas_call | solution.py:221
  203.1 11.3 %grad_one.1 = f32[2304,256]{1,0:T(8,128)} custom-call(s32[48]{0:T(128)} %reshape.111.refs_0_, s32[48]{0:T(128)} %reshape.99.refs_1_, bf16[384,16,256]{2,1,0:T(8,128)(2,1)} %bitcast.33, bf16[12,16,16,256]{3,2,1,0:T(8,128)(2,1)} %get-tuple-element.31.refs_3_, f32[12,256,256]{2,1,0:T(8,128)} %get-tuple-element.32.refs_4_, ...), custom_call_target="tpu_custom_call" | custom-call | tf_op jit(solution)/shard_map/grad_one/pallas_call | solution.py:627
  214.4 43.6 %scatter.1 = (f32[72,256]{1,0:T(8,128)}, f32[72,256]{1,0:T(8,128)}, f32[8,128]{1,0:T(8,128)}) custom-call(f32[4,2,4,72,256]{4,3,2,1,0:T(8,128)} %bitcast.35, f32[4,2,4,72,256]{4,3,2,1,0:T(8,128)} %bitcast.34, f32[4,2,4,8,128]{4,3,2,1,0:T(8,128)} %bitcast.44), custom_call_target="tpu_custom_call" | custom-call | tf_op jit(solution)/shard_map/scatter/pallas_call | solution.py:332
  258.1 0.9 pad_maximum_fusion.1
  259.0 0.7 copy.59
  259.7 1.3 copy.73
  (7 shorter events, 0.1 us)
Async XLA Ops:
  169.5 8.7 %copy-start = (f32[80,256]{1,0:T(8,128)S(1)}, f32[80,256]{1,0:T(8,128)}, u32[]{:S(2)}) copy-start(f32[80,256]{1,0:T(8,128)} %get-tuple-element.36) | copy-start | bytes 245764

commit v2 on v1

--- a/solution.py
+++ b/solution.py
@@ -133,6 +133,13 @@
         self.forward(0).start()
 
     def relay(self):
+        self.relay_first()
+        self.relay_rest()
+
+    def relay_first(self):
+        pass
+
+    def relay_rest(self):
         for j in range(1, self.chips):
             self.direct(j).wait_recv()
             self.forward(j).start()
@@ -144,27 +151,105 @@
             self.forward(j).wait()
 
 
+class SquareGather:
+    def __init__(self, src, out, chips, sems):
+        self.src, self.out = src, out
+        self.send, self.recv, self.fsend, self.frecv = sems
+        face = lax.axis_index("face")
+        core, chip = face % 2, face // 2
+        col, row = chip % 2, chip // 2
+        self.face = face
+        self.partner = chip * 2 + 1 - core
+        self.beside = (row * 2 + 1 - col) * 2 + core
+        self.below = ((1 - row) * 2 + col) * 2 + core
+        self.across = ((1 - row) * 2 + 1 - col) * 2 + core
+        self.half = src.shape[0] // 2
+
+    def part(self, k):
+        return pl.ds((0, 1, 1, 0, 0, 1)[k] * self.half, self.half)
+
+    def came(self, k):
+        block = (self.beside, self.beside, self.below, self.below, self.across, self.across)[k]
+        return self.out.at[block, self.part(k)]
+
+    def direct(self, k):
+        to = (self.beside, self.beside, self.below, self.below, self.below, self.beside)[k]
+        if k < 4:
+            src, block = self.src.at[self.part(k)], self.face
+        else:
+            block = self.beside if k == 4 else self.below
+            src = self.out.at[block, self.part(k)]
+        return rcopy(
+            src, self.out.at[block, self.part(k)], self.send.at[k], self.recv.at[k], face=to
+        )
+
+    def forward(self, k):
+        if k == 6:
+            src, dst = self.src, self.out.at[self.face]
+        else:
+            src = dst = self.came(k)
+        return rcopy(src, dst, self.fsend.at[k], self.frecv.at[k], face=self.partner)
+
+    def start(self):
+        for k in (0, 2, 1, 3):
+            self.direct(k).start()
+        self.forward(6).start()
+
+    def relay(self):
+        self.relay_first()
+        self.relay_rest()
+
+    def relay_first(self):
+        for k, onward in ((0, 4), (2, 5)):
+            self.direct(k).wait_recv()
+            self.direct(onward).start()
+            self.forward(k).start()
+
+    def relay_rest(self):
+        for k in (1, 3, 4, 5):
+            self.direct(k).wait_recv()
+            self.forward(k).start()
+
+    def finish(self):
+        for k in range(6):
+            self.direct(k).wait_send()
+        for k in range(7):
+            self.forward(k).wait()
+
+
+def gather_over_face(src, out, chips, sems):
+    kind = SquareGather if chips == 4 and src.shape[0] % 2 == 0 else FaceGather
+    return kind(src, out, chips, sems)
+
+
 def dma_sems(*sizes):
     return [pltpu.SemaphoreType.DMA((max(n, 1),)) for n in sizes]
 
 
 def first_gather_kernel(chips, members, count, *refs):
-    edges, ws = refs[0], refs[1 : 1 + count]
+    x, ws = refs[0], refs[1 : 1 + count]
     edges_out, outs = refs[1 + count], refs[2 + count : 2 + 2 * count]
-    sems = refs[2 + 2 * count :]
-    own_sem, sems = sems[0], sems[1:]
+    edges, field, own_sem = refs[2 + 2 * count : 5 + 2 * count]
+    sems = refs[5 + 2 * count :]
     face = lax.axis_index("face")
     member = lax.axis_index("member")
-    own = [pltpu.make_async_copy(edges, edges_out.at[face], own_sem.at[0])]
+    own = []
     for k in range(count):
         own.append(
             pltpu.make_async_copy(ws[k], outs[k].at[face, member], own_sem.at[k + 1])
         )
-    for c in own:
-        c.start()
+        own[k].start()
+
+    def cut(k, carry):
+        field[...] = x[k].astype(f32)
+        sides_out(field, edges, k)
+        return carry
+
+    lax.fori_loop(0, x.shape[0], cut, 0)
     greet(chips, members, True, True)
-    eg = FaceGather(edges, edges_out, chips, sems[:4])
+    eg = gather_over_face(edges, edges_out, chips, sems[:4])
     eg.start()
+    edges_out[face] = edges[...]
     for c in own:
         c.wait()
     rest = sems[4:]
@@ -172,10 +257,12 @@
     for k in range(count):
         line = rest[8 * k : 8 * k + 4]
         line_gather(ws[k], lambda b: outs[k].at[face, b], member, members, line)
-        wg = FaceGather(outs[k].at[face], outs[k], chips, rest[8 * k + 4 : 8 * k + 8])
+        wg = gather_over_face(outs[k].at[face], outs[k], chips, rest[8 * k + 4 : 8 * k + 8])
         wg.start()
         wgs.append(wg)
-    eg.relay()
+        if k == 0:
+            eg.relay_first()
+    eg.relay_rest()
     for wg in wgs:
         wg.relay()
     eg.finish()
@@ -183,33 +270,35 @@
         wg.finish()
 
 
-def first_gather(edges, ws, faces, members):
+def first_gather(x, ws, faces, members):
     chips = faces // 2
     count = len(ws)
-    shapes = [jax.ShapeDtypeStruct((faces,) + edges.shape, edges.dtype)] + [
-        jax.ShapeDtypeStruct((faces, members) + w.shape, w.dtype) for w in ws
+    n, h, w, c = x.shape
+    shapes = [jax.ShapeDtypeStruct((faces, n, 4, w, c), x.dtype)] + [
+        jax.ShapeDtypeStruct((faces, members) + v.shape, v.dtype) for v in ws
     ]
-    sems = dma_sems(count + 1) + dma_sems(*([chips] * 4))
+    scratch = [VMEM((n, 4, w, c), x.dtype), VMEM((h, w, c), f32)]
+    scratch += dma_sems(count + 1) + dma_sems(*([chips + 3] * 4))
     for _ in ws:
-        sems += dma_sems(*([members] * 4)) + dma_sems(*([chips] * 4))
+        scratch += dma_sems(*([members] * 4)) + dma_sems(*([chips + 3] * 4))
     return pl.pallas_call(
         functools.partial(first_gather_kernel, chips, members, count),
         out_shape=shapes,
         in_specs=[pl.BlockSpec(memory_space=VMEM)] * (count + 1),
         out_specs=[pl.BlockSpec(memory_space=VMEM)] * (count + 1),
-        scratch_shapes=sems,
+        scratch_shapes=scratch,
         compiler_params=pltpu.CompilerParams(
             collective_id=1, has_side_effects=True, vmem_limit_bytes=LIMIT
         ),
         name="first_gather",
-    )(edges, *ws)
+    )(x, *ws)
 
 
 def face_gather_kernel(chips, x, out, own_sem, *sems):
     own = pltpu.make_async_copy(x, out.at[lax.axis_index("face")], own_sem.at[0])
     own.start()
     greet(chips, 1, True, False)
-    g = FaceGather(x, out, chips, sems)
+    g = gather_over_face(x, out, chips, sems)
     g.start()
     own.wait()
     g.relay()
@@ -223,7 +312,7 @@
         out_shape=jax.ShapeDtypeStruct((faces,) + x.shape, x.dtype),
         in_specs=[pl.BlockSpec(memory_space=VMEM)],
         out_specs=pl.BlockSpec(memory_space=VMEM),
-        scratch_shapes=dma_sems(1) + dma_sems(*([chips] * 4)),
+        scratch_shapes=dma_sems(1) + dma_sems(*([chips + 3] * 4)),
         compiler_params=pltpu.CompilerParams(
             collective_id=ident, has_side_effects=True, vmem_limit_bytes=LIMIT
         ),
@@ -231,27 +320,117 @@
     )(x)
 
 
-def member_gather_kernel(members, x, out, own_sem, *sems):
+def score_kernel(members, held, tile_dev, chunk, h, *refs):
+    y, obs, out, packed, came, slopes, back = refs[:7]
+    s1, r1, s2, r2 = refs[7:]
     member = lax.axis_index("member")
-    own = pltpu.make_async_copy(x, out.at[member], own_sem.at[0])
-    own.start()
+    part = obs.shape[-1]
+    ensemble = held * members
+    chunks = tile_dev // chunk
+
+    def there(j):
+        return (member + j) % members
+
+    def source(j):
+        return (member + members - j) % members
+
+    def go(i, j):
+        at = pl.ds(i * chunk, chunk)
+        return rcopy(
+            packed.at[there(j), at], came.at[j, at], s1.at[i, j], r1.at[i, j], member=there(j)
+        )
+
+    def home(i, j):
+        at = pl.ds(i * chunk, chunk)
+        return rcopy(
+            slopes.at[j, at], back.at[member, at], s2.at[i, j], r2.at[i, j], member=source(j)
+        )
+
+    def home_here(i, j):
+        at = pl.ds(i * chunk, chunk)
+        return rcopy(
+            slopes.at[j, at], back.at[there(j), at], s2.at[i, j], r2.at[i, j], member=source(j)
+        )
+
+    def pack(t):
+        for q in range(members):
+            packed[q, t] = jnp.concatenate(
+                [y[m * tile_dev + t][:, q * part : (q + 1) * part] for m in range(held)], axis=1
+            )
+
+    def g(v):
+        return v * lax.rsqrt(v * v + smooth_sq)
+
+    def score(t):
+        o = obs[t].astype(f32)
+        o = jnp.concatenate([o] * held, axis=1)
+        vals = [packed[member, t].astype(f32)]
+        vals += [came[j, t].astype(f32) for j in range(1, members)]
+        turned = [
+            jnp.concatenate([v[:, k * part :], v[:, : k * part]], axis=1) if k else v
+            for v in vals
+            for k in range(held)
+        ]
+        for j in range(members):
+            v = vals[j]
+            paired = jnp.zeros_like(v)
+            for u in turned:
+                paired = paired + g(v - u)
+            s = (g(v - o) / ensemble - paired / (ensemble * ensemble)) / h
+            s = s.astype(bf16)
+            if j == 0:
+                back[member, t] = s
+            else:
+                slopes[j, t] = s
+
+    pack_first = [pack(t) for t in range(chunk)]
+    del pack_first
     greet(1, members, False, True)
-    line_gather(x, lambda b: out.at[b], member, members, sems)
-    own.wait()
-
-
-def member_gather(x, members, ident):
+    for i in range(chunks):
+        if i:
+            for t in range(i * chunk, (i + 1) * chunk):
+                pack(t)
+        for j in range(1, members):
+            go(i, j).start()
+    for i in range(chunks):
+        for j in range(1, members):
+            go(i, j).wait_recv()
+        for t in range(i * chunk, (i + 1) * chunk):
+            score(t)
+        for j in range(1, members):
+            home(i, j).start()
+    for i in range(chunks):
+        for j in range(1, members):
+            home_here(i, j).wait_recv()
+        for t in range(i * chunk, (i + 1) * chunk):
+            for m in range(held):
+                out[m * tile_dev + t] = jnp.concatenate(
+                    [back[q, t][:, m * part : (m + 1) * part] for q in range(members)], axis=1
+                )
+    for i in range(chunks):
+        for j in range(1, members):
+            go(i, j).wait_send()
+            home(i, j).wait_send()
+
+
+def score_exchange(y, obs, members, h, ident):
+    n, variables, cells = y.shape
+    tile_dev = obs.shape[0]
+    held = n // tile_dev
+    chunk = 2 if tile_dev % 2 == 0 else 1
+    wide = (members, tile_dev, variables, held * obs.shape[-1])
+    sems = pltpu.SemaphoreType.DMA((tile_dev // chunk, members))
     return pl.pallas_call(
-        functools.partial(member_gather_kernel, members),
-        out_shape=jax.ShapeDtypeStruct((members,) + x.shape, x.dtype),
-        in_specs=[pl.BlockSpec(memory_space=VMEM)],
+        functools.partial(score_kernel, members, held, tile_dev, chunk, h),
+        out_shape=jax.ShapeDtypeStruct(y.shape, bf16),
+        in_specs=[pl.BlockSpec(memory_space=VMEM)] * 2,
         out_specs=pl.BlockSpec(memory_space=VMEM),
-        scratch_shapes=dma_sems(1) + dma_sems(*([members] * 4)),
+        scratch_shapes=[VMEM(wide, bf16)] * 4 + [sems] * 4,
         compiler_params=pltpu.CompilerParams(
             collective_id=ident, has_side_effects=True, vmem_limit_bytes=LIMIT
         ),
-        name="member_gather",
-    )(x)
+        name="score",
+    )(y, obs)
 
 
 def scatter_kernel(chips, members, count, *refs):
@@ -379,14 +558,46 @@
     return s * (1.0 + v * (1.0 - s))
 
 
-def conv_kernel(block, last, *refs):
-    index_ref, flip_ref, x_ref, edges_ref, w_ref = refs[:5]
+def table(place_ref, glue_ref, index_ref, flip_ref, slot_of, members, tile_dev):
+    first = lax.axis_index("face") * tile_dev
+
+    def invert(s, carry):
+        slot_of[place_ref[s]] = s
+        return carry
+
+    lax.fori_loop(0, place_ref.shape[0], invert, 0)
+
+    def fill(i, carry):
+        tile = place_ref[first + i]
+        for a in range(4):
+            base = (tile * 4 + a) * 3
+            slot = slot_of[glue_ref[base]]
+            face = slot // tile_dev
+            inner = slot - face * tile_dev
+            for m in range(members):
+                at = (m * tile_dev + i) * 4 + a
+                index_ref[at] = ((face * members + m) * tile_dev + inner) * 4 + glue_ref[base + 1]
+                flip_ref[at] = glue_ref[base + 2]
+        return carry
+
+    lax.fori_loop(0, tile_dev, fill, 0)
+
+
+def conv_kernel(block, members, *refs):
+    last = members is None
     if last:
+        index_ref, flip_ref, x_ref, edges_ref, w_ref = refs[:5]
         head_ref, x3_ref, pre_ref, act_ref, out_ref, pad = refs[5:]
     else:
-        x3_ref, pre_ref, act_ref, side_ref, pad, field = refs[5:]
+        place_ref, glue_ref, x_ref, edges_ref, w_ref = refs[:5]
+        x3_ref, pre_ref, act_ref, side_ref, index_ref, flip_ref, pad, field, slot_of = refs[5:]
     _, h, w, c = x_ref.shape
     step = pl.program_id(0)
+    if not last:
+        tile_dev = index_ref.shape[0] // (4 * members)
+        pl.when(step == 0)(
+            lambda: table(place_ref, glue_ref, index_ref, flip_ref, slot_of, members, tile_dev)
+        )
     for k in range(block):
         n = step * block + k
         rims = rims_of(index_ref, flip_ref, edges_ref, n, w)
@@ -435,23 +646,27 @@
     return 3 if n % 3 == 0 else (2 if n % 2 == 0 else 1)
 
 
-def conv(index, flips, x, edges, w, head_t=None):
+def layer(shape, which):
+    return pl.BlockSpec((shape[0], shape[1] // 2), lambda i: (0, which))
+
+
+def conv(scalars, x, edges, w, members=None, head_t=None):
     n, h, wd, c = x.shape
     block = block_of(n)
-    last = head_t is not None
+    last = members is None
     in_specs = [
         SMEM_SPEC,
         SMEM_SPEC,
         tiles(block, (h, wd, c)),
         whole(edges.shape),
-        whole(w.shape),
+        layer(w.shape, int(last)),
     ]
     shapes = [
         jax.ShapeDtypeStruct((n, h + 2, wd, 3 * c), bf16),
         jax.ShapeDtypeStruct((n, h * wd, c), f32),
         jax.ShapeDtypeStruct((n, h * wd, c) if last else (n, h, wd, c), bf16),
     ]
-    args = [index, flips, x, edges, w]
+    args = [*scalars, x, edges, w]
     scratch = [VMEM((h + 2, wd + 16, c), f32)]
     if last:
         in_specs.append(whole(head_t.shape))
@@ -460,21 +675,26 @@
     else:
         shapes.append(jax.ShapeDtypeStruct((n, 4, wd, c), bf16))
         scratch.append(VMEM((h, wd, c), f32))
+        scratch.append(pltpu.SMEM(scalars[0].shape, jnp.int32))
+    out_specs = [tiles(block, s.shape[1:]) for s in shapes]
+    if not last:
+        shapes += [jax.ShapeDtypeStruct((n * 4,), jnp.int32)] * 2
+        out_specs += [SMEM_SPEC] * 2
     return pl.pallas_call(
-        functools.partial(conv_kernel, block, last),
+        functools.partial(conv_kernel, block, members),
         grid=(n // block,),
         out_shape=shapes,
         in_specs=in_specs,
-        out_specs=[tiles(block, s.shape[1:]) for s in shapes],
+        out_specs=out_specs,
         scratch_shapes=scratch,
         compiler_params=pltpu.CompilerParams(vmem_limit_bytes=LIMIT),
         name="conv_last" if last else "conv_first",
     )(*args)
 
 
-def back_kernel(block, ensemble, tile_dev, h, w, *refs):
-    y_ref, own_ref, obs_ref, act_ref, pre_ref, head_ref, w_ref = refs[:7]
-    slope_ref, inner_ref, side_ref, hg_ref, va, vb, pad, s3, cols = refs[7:]
+def back_kernel(block, h, w, *refs):
+    out_ref, act_ref, pre_ref, head_ref, w_ref = refs[:5]
+    slope_ref, inner_ref, side_ref, hg_ref, va, vb, pad, s3, cols = refs[5:]
     c = act_ref.shape[-1]
     step = pl.program_id(0)
 
@@ -492,17 +712,7 @@
         pad[...] = jnp.zeros_like(pad)
 
     for k in range(block):
-        t = (step * block + k) % tile_dev
-        y = own_ref[k].astype(f32)
-
-        def g(x):
-            return x * lax.rsqrt(x * x + smooth_sq)
-
-        gap = g(y - obs_ref[t].astype(f32))
-        paired = jnp.zeros_like(y)
-        for m in range(ensemble):
-            paired = paired + g(y - y_ref[m, t].astype(f32))
-        slope_out = ((gap / ensemble - paired / (ensemble * ensemble)) / h).astype(bf16)
+        slope_out = out_ref[k]
         hg_ref[...] += mm(slope_out, act_ref[k])
         back = mm(slope_out, head_ref[...], TN)
         slope = (back * dsilu(pre_ref[k])).astype(bf16)
@@ -530,9 +740,8 @@
         side_ref[k, 3] = lefts[k * h : (k + 1) * h]
 
 
-def backward(y_all, own, obs, act, pre, head_t, w, h, wd):
+def backward(slope_out, act, pre, head_t, w, h, wd):
     n, cells, c = act.shape
-    ensemble, tile_dev = y_all.shape[:2]
     block = block_of(n)
     shapes = [
         jax.ShapeDtypeStruct((n, cells, c), bf16),
@@ -541,17 +750,15 @@
         jax.ShapeDtypeStruct(head_t.shape, f32),
     ]
     return pl.pallas_call(
-        functools.partial(back_kernel, block, ensemble, tile_dev, h, wd),
+        functools.partial(back_kernel, block, h, wd),
         grid=(n // block,),
         out_shape=shapes,
         in_specs=[
-            whole(y_all.shape),
-            tiles(block, own.shape[1:]),
-            whole(obs.shape),
+            tiles(block, slope_out.shape[1:]),
             tiles(block, (cells, c)),
             tiles(block, (cells, c)),
             whole(head_t.shape),
-            whole(w.shape),
+            layer(w.shape, 1),
         ],
         out_specs=[tiles(block, s.shape[1:]) for s in shapes[:3]] + [whole(head_t.shape)],
         scratch_shapes=[
@@ -563,7 +770,7 @@
         ],
         compiler_params=pltpu.CompilerParams(vmem_limit_bytes=LIMIT),
         name="backward",
-    )(y_all, own, obs, act, pre, head_t, w)
+    )(slope_out, act, pre, head_t, w)
 
 
 def grad_kernel(block, steps, mid, h, w, *refs):
@@ -636,58 +843,32 @@
     )(*args)
 
 
-def split_edges(x):
-    return jnp.stack([x[:, 0], x[:, :, -1], x[:, -1], x[:, :, 0]], axis=1)
-
-
-def edge_table(adjacency, placement_map, first_slot, members, tile_dev):
-    total = placement_map.shape[0]
-    ids = jnp.arange(total, dtype=jnp.int32)
-    mine = first_slot + jnp.arange(tile_dev, dtype=jnp.int32)
-    my_tiles = jnp.sum(jnp.where(ids[None] == mine[:, None], placement_map[None], 0), axis=1)
-    hit = ids[None, :] == my_tiles[:, None]
-    entries = jnp.sum(jnp.where(hit[:, :, None, None], adjacency[None], 0), axis=1)
-    neighbour, side, flip = entries[:, :, 0], entries[:, :, 1], entries[:, :, 2]
-    found = neighbour[:, :, None] == placement_map[None, None, :]
-    slot = jnp.sum(jnp.where(found, ids[None, None, :], 0), axis=2)
-    face, inner = slot // tile_dev, slot % tile_dev
-    m = jnp.arange(members, dtype=jnp.int32)[:, None, None]
-    index = ((face[None] * members + m) * tile_dev + inner[None]) * 4 + side[None]
-    flips = jnp.broadcast_to(flip[None], index.shape)
-    return index.reshape(-1), flips.reshape(-1)
-
-
 def shards(faces, zs, features, observed, conv_weights, head_weight, adjacency, placement_map):
     members, tile_dev, h, w, c = features.shape
     n = members * tile_dev
     variables = head_weight.shape[1]
-    index, flips = edge_table(
-        adjacency, placement_map, lax.axis_index("face") * tile_dev, members, tile_dev
-    )
     x = features.reshape(n, h, w, c)
     rows = conv_weights.shape[0]
     head_rows = head_weight.shape[0]
     lanes = -(-variables // 128) * 128
     head_wide = jnp.pad(head_weight, ((0, 0), (0, lanes - variables)))
-    edges, w0, w1, head = first_gather(
-        split_edges(x), [conv_weights[:, 0], conv_weights[:, 1], head_wide], faces, zs
+    edges, weights, head = first_gather(
+        x, [conv_weights.reshape(rows, 2 * c), head_wide], faces, zs
     )
-    w0 = w0.reshape(faces * zs * rows, c)
-    w1 = w1.reshape(faces * zs * rows, c)
+    weights = weights.reshape(faces * zs * rows, 2 * c)
     head_t = head.reshape(faces * zs * head_rows, lanes)[:, :variables].T
-    obs = lax.all_gather(observed, "member", axis=2, tiled=True)
 
     def flat(e):
         return e.reshape((faces * n * 4,) + e.shape[-2:])
 
-    x3_one, pre_one, act_one, sides = conv(index, flips, x, flat(edges), w0)
+    x3_one, pre_one, act_one, sides, index, flips = conv(
+        (placement_map, adjacency.reshape(-1)), x, flat(edges), weights, members=members
+    )
     x3_two, pre_two, act_two, outs = conv(
-        index, flips, act_one, flat(face_gather(sides, faces, 2)), w1, head_t
+        (index, flips), act_one, flat(face_gather(sides, faces, 2)), weights, head_t=head_t
     )
-    y_all = member_gather(outs, zs, 3).reshape(zs * members, tile_dev, variables, h * w)
-    slope_two, inner, borders, hg = backward(
-        y_all, outs, obs, act_two, pre_two, head_t, w1, h, w
-    )
+    slope_out = score_exchange(outs, observed, zs, h, 3)
+    slope_two, inner, borders, hg = backward(slope_out, act_two, pre_two, head_t, weights, h, w)
     grad_two = weight_grad(x3_two, h, w, c, slope=slope_two)
     returned = flat(face_gather(borders, faces, 4))
     grad_one = weight_grad(x3_one, h, w, c, mid=(index, flips, returned, inner, pre_one))

time: 262 us -> 214 us (0.82)
  Pallas kernels: 226 us -> 203 us
  blocking collectives: 16.5 us -> 0 us
  local copies, waits for them, and re-layouts: 12.7 us -> 8.67 us
  other arithmetic: 4.66 us -> 0.93 us
    all_gather x1 -> x0, blocking collectives: 16.5 us -> none  [shards(): obs = lax.all_gather(observed, 'member', axis=2, tiled=True)]
    pallas_call x4, Pallas kernels: 74.6 us -> 58.6 us  [the longest x1 27.8 us: score_exchange(): pl.pallas_call(functools.partial(score_kernel, members, held, tile_dev, c...]
    pallas_call x2, Pallas kernels: 48.9 us -> 40.9 us  [face_gather(): pl.pallas_call(functools.partial(face_gather_kernel, chips), out_shape=ja...]
    slice x7 -> x0, local copies, waits for them, and re-layouts: 4.09 us -> none  [the longest x2 2.72 us: split_edges(): return jnp.stack([x[:, 0], x[:, :, -1], x[:, -1], x[:, :, 0]], axis=1)]
    reduce_sum x3 -> x0, other arithmetic: 2.81 us -> none  [the longest x1 1.07 us: edge_table(): jnp.sum(jnp.where(hit[:, :, None, None], adjacency[None], 0), axis=1)]
    unnamed x8 -> x13, local copies, waits for them, and re-layouts: 3.67 us -> 5.92 us
where the time goes in v2:
time: 214 us; the launch traced here: 213 us
  Pallas kernels  203 us (95%)
  local copies, waits for them, and re-layouts  8.67 us (4%)
    pallas_call x1, Pallas kernels, scatter(): pl.pallas_call(functools.partial(scatter_kernel, chips, members, len(gs))...  43.7 us
    pallas_call x2, Pallas kernels, face_gather(): pl.pallas_call(functools.partial(face_gather_kernel, chips), out_shape=ja...  40.9 us
    pallas_call x1, Pallas kernels, first_gather(): pl.pallas_call(functools.partial(first_gather_kernel, chips, members, cou...  39.4 us
    pallas_call x1, Pallas kernels, score_exchange(): pl.pallas_call(functools.partial(score_kernel, members, held, tile_dev, c...  27.8 us
    pallas_call x2, Pallas kernels, conv(): pl.pallas_call(functools.partial(conv_kernel, block, members), grid=(n //...  20.3 us
    pallas_call x2, Pallas kernels, weight_grad(): pl.pallas_call(functools.partial(grad_kernel, block, steps, mid is not No...  20.2 us
    pallas_call x1, Pallas kernels, backward(): pl.pallas_call(functools.partial(back_kernel, block, h, wd), grid=(n // b...  10.5 us
    unnamed x13, local copies, waits for them, and re-layouts  5.92 us

profile of v2, /device:TPU:0, one launch (start us, length us, event | category | flops | bytes accessed | tf_op | source)
XLA Modules:
  0.0 213.0 jit_solution(12672296249909346062)
XLA Ops:
  0.6 1.5 copy.19
  2.2 1.3 pad.8.refs_2_
  3.4 39.4 %first_gather.1 = (bf16[8,12,4,16,256]{4,3,2,1,0:T(8,128)(2,1)}, bf16[8,4,72,512]{3,2,1,0:T(8,128)(2,1)}, bf16[8,4,8,128]{3,2,1,0:T(8,128)(2,1)}) custom-call(bf16[12,16,16,256]{3,2,1,0:T(8,128)(2,1)} %bitcast.24, bf16[72,512]{1,0:T(8,128)(2,1)} %bitcast.30, bf16[8,128]{1,0:T(8,128)(2,1)} %pad.8.refs_2_), custom_call_target="tpu_custom_call" | custom-call | tf_op jit(solution)/shard_map/first_gather/pallas_call | solution.py:284
  42.8 0.8 copy.12
  43.6 0.8 reshape.37.refs_1_
  44.4 10.7 %conv_first.1 = (bf16[12,18,16,768]{3,2,1,0:T(8,128)(2,1)}, f32[12,256,256]{2,1,0:T(8,128)}, bf16[12,16,16,256]{3,2,1,0:T(8,128)(2,1)}, bf16[12,4,16,256]{3,2,1,0:T(8,128)(2,1)}, s32[48]{0:T(128)}, /*index=5*/s32[48]{0:T(128)}) custom-call(s32[48]{0:T(128)} %refs_0_.1, s32[576]{0:T(1024)} %reshape.37.refs_1_, bf16[12,16,16,256]{3,2,1,0:T(8,128)(2,1)} %bitcast.25, ...), custom_call_target="tpu_custom_call" | custom-call | tf_op jit(solution)/shard_map/conv_first/pallas_call | solution.py:683
  55.1 0.0 copy-start.2
  55.1 21.9 %face_gather.2 = bf16[8,12,4,16,256]{4,3,2,1,0:T(8,128)(2,1)} custom-call(bf16[12,4,16,256]{3,2,1,0:T(8,128)(2,1)} %get-tuple-element.27.x), custom_call_target="tpu_custom_call" | custom-call | tf_op jit(solution)/shard_map/face_gather/pallas_call | solution.py:310
  77.1 0.0 copy-done.2
  77.1 0.7 copy.17
  77.8 0.0 copy-start
  77.8 9.5 %conv_last.1 = (bf16[12,18,16,768]{3,2,1,0:T(8,128)(2,1)}, f32[12,256,256]{2,1,0:T(8,128)}, bf16[12,256,256]{2,1,0:T(8,128)(2,1)}, bf16[12,80,256]{2,1,0:T(8,128)(2,1)}) custom-call(s32[48]{0:T(128)} %get-tuple-element.24.refs_0_, s32[48]{0:T(128)} %get-tuple-element.25.refs_1_, bf16[12,16,16,256]{3,2,1,0:T(8,128)(2,1)} %get-tuple-element.26.refs_2_, ...), custom_call_target="tpu_custom_call" | custom-call | tf_op jit(solution)/shard_map/conv_last/pallas_call | solution.py:683
  87.3 0.0 copy-done
  87.3 0.8 copy.14.refs_1_
  88.1 27.8 %score.1.refs_0_ = bf16[12,80,256]{2,1,0:T(8,128)(2,1)} custom-call(bf16[12,80,256]{2,1,0:T(8,128)(2,1)} %get-tuple-element.29.refs_0_, bf16[6,80,64]{2,1,0:T(8,128)(2,1)} %copy.14.refs_1_), custom_call_target="tpu_custom_call" | custom-call | tf_op jit(solution)/shard_map/score/pallas_call | solution.py:423
  115.9 10.5 %backward.1 = (bf16[12,256,256]{2,1,0:T(8,128)(2,1)}, bf16[12,16,16,256]{3,2,1,0:T(8,128)(2,1)}, bf16[12,4,16,256]{3,2,1,0:T(8,128)(2,1)}, f32[80,256]{1,0:T(8,128)}) custom-call(bf16[12,80,256]{2,1,0:T(8,128)(2,1)} %score.1.refs_0_, bf16[12,256,256]{2,1,0:T(8,128)(2,1)} %get-tuple-element.30.refs_1_, f32[12,256,256]{2,1,0:T(8,128)} %get-tuple-element.31.refs_2_, ...), custom_call_target="tpu_custom_call" | custom-call | tf_op jit(solution)/shard_map/backward/pallas_call | solution.py:752
  126.4 8.6 %grad_two.1 = f32[2304,256]{1,0:T(8,128)} custom-call(bf16[12,256,256]{2,1,0:T(8,128)(2,1)} %get-tuple-element.36.refs_0_, bf16[12,18,16,768]{3,2,1,0:T(8,128)(2,1)} %get-tuple-element.37.refs_1_), custom_call_target="tpu_custom_call" | custom-call | tf_op jit(solution)/shard_map/grad_two/pallas_call | solution.py:834
  135.0 19.0 %face_gather.3 = bf16[8,12,4,16,256]{4,3,2,1,0:T(8,128)(2,1)} custom-call(bf16[12,4,16,256]{3,2,1,0:T(8,128)(2,1)} %get-tuple-element.32.x), custom_call_target="tpu_custom_call" | custom-call | tf_op jit(solution)/shard_map/face_gather/pallas_call | solution.py:310
  154.1 0.0 copy-start.1
  154.1 11.5 %grad_one.1 = f32[2304,256]{1,0:T(8,128)} custom-call(s32[48]{0:T(128)} %get-tuple-element.24.refs_0_, s32[48]{0:T(128)} %get-tuple-element.25.refs_1_, bf16[384,16,256]{2,1,0:T(8,128)(2,1)} %bitcast.21, bf16[12,16,16,256]{3,2,1,0:T(8,128)(2,1)} %get-tuple-element.33.refs_3_, f32[12,256,256]{2,1,0:T(8,128)} %get-tuple-element.34.refs_4_, ...), custom_call_target="tpu_custom_call" | custom-call | tf_op jit(solution)/shard_map/grad_one/pallas_call | solution.py:834
  165.7 0.0 copy-done.1
  165.7 0.1 copy.18
  165.7 0.7 pad.9.clone
  166.4 43.7 %scatter.1 = (f32[72,256]{1,0:T(8,128)}, f32[72,256]{1,0:T(8,128)}, f32[8,128]{1,0:T(8,128)}) custom-call(f32[4,2,4,72,256]{4,3,2,1,0:T(8,128)} %bitcast.23, f32[4,2,4,72,256]{4,3,2,1,0:T(8,128)} %bitcast.22, f32[4,2,4,8,128]{4,3,2,1,0:T(8,128)} %bitcast.27), custom_call_target="tpu_custom_call" | custom-call | tf_op jit(solution)/shard_map/scatter/pallas_call | solution.py:511
  210.1 0.9 pad_maximum_fusion
  211.0 0.7 copy.16
  211.8 1.3 copy.21
Async XLA Ops:
  55.1 21.9 %copy-start.2 = (bf16[8,4,8,128]{3,2,1,0:T(8,128)(2,1)S(1)}, bf16[8,4,8,128]{3,2,1,0:T(8,128)(2,1)}, u32[]{:S(2)}) copy-start(bf16[8,4,8,128]{3,2,1,0:T(8,128)(2,1)} %get-tuple-element.28) | copy-start | bytes 196612
  77.8 9.5 %copy-start = (bf16[6,80,64]{1,2,0:T(8,128)(2,1)S(1)}, bf16[6,80,64]{1,2,0:T(8,128)(2,1)}, u32[]{:S(2)}) copy-start(bf16[6,80,64]{1,2,0:T(8,128)(2,1)} %param.7) | copy-start | bytes 184324
  154.1 11.6 %copy-start.1 = (f32[80,256]{1,0:T(8,128)S(1)}, f32[80,256]{1,0:T(8,128)}, u32[]{:S(2)}) copy-start(f32[80,256]{1,0:T(8,128)} %get-tuple-element.38) | copy-start | bytes 245764

commit v3 on v2

--- a/solution.py
+++ b/solution.py
@@ -433,92 +433,85 @@
     )(y, obs)
 
 
-def scatter_kernel(chips, members, count, *refs):
-    gs, outs = refs[:count], refs[count : 2 * count]
-    scratch = refs[2 * count :]
-    face = lax.axis_index("face")
-    member = lax.axis_index("member")
-    core, chip = face % 2, face // 2
-    partner = chip * 2 + 1 - core
-    greet(chips, members, True, True)
-
-    def parts(k):
-        return scratch[10 * k : 10 * k + 10]
-
-    def there(j):
-        return (chip + j) % chips
-
-    def core_copy(k, j):
-        fromcore, _, _, _, s0, r0, _, _, _, _ = parts(k)
-        return rcopy(
-            gs[k].at[there(j), 1 - core], fromcore.at[j], s0.at[j], r0.at[j], face=partner
-        )
-
-    def chip_copy(k, j):
-        _, acc, fromchip, _, _, _, s1, r1, _, _ = parts(k)
-        return rcopy(acc.at[j], fromchip.at[j], s1.at[j], r1.at[j], face=there(j) * 2 + core)
-
-    def line_copy(k, j):
-        _, acc, _, fromline, _, _, _, _, s2, r2 = parts(k)
-        to = (member + j) % members
-        return rcopy(acc.at[0, to], fromline.at[j], s2.at[j], r2.at[j], member=to)
-
-    order = list(range(1, chips)) + [0]
-    for k in range(count):
-        for j in order:
-            core_copy(k, j).start()
-    for k in range(count):
-        fromcore, acc = parts(k)[:2]
-        for j in order:
-            core_copy(k, j).wait_recv()
-            acc[j] = gs[k][there(j), core] + fromcore[j]
+class Scatter:
+    def __init__(self, g, out, chips, members, scratch):
+        self.g, self.out, self.chips, self.members = g, out, chips, members
+        self.fromcore, self.acc, self.fromchip, self.fromline = scratch[:4]
+        self.s0, self.r0, self.s1, self.r1, self.s2, self.r2 = scratch[4:]
+        face = lax.axis_index("face")
+        self.member = lax.axis_index("member")
+        self.core, self.chip = face % 2, face // 2
+        self.partner = self.chip * 2 + 1 - self.core
+        self.order = list(range(1, chips)) + [0]
+
+    def there(self, j):
+        return (self.chip + j) % self.chips
+
+    def core_copy(self, j):
+        return rcopy(
+            self.g.at[self.there(j), 1 - self.core],
+            self.fromcore.at[j],
+            self.s0.at[j],
+            self.r0.at[j],
+            face=self.partner,
+        )
+
+    def chip_copy(self, j):
+        return rcopy(
+            self.acc.at[j],
+            self.fromchip.at[j],
+            self.s1.at[j],
+            self.r1.at[j],
+            face=self.there(j) * 2 + self.core,
+        )
+
+    def line_copy(self, j):
+        to = (self.member + j) % self.members
+        return rcopy(
+            self.acc.at[0, to], self.fromline.at[j], self.s2.at[j], self.r2.at[j], member=to
+        )
+
+    def core_start(self):
+        for j in self.order:
+            self.core_copy(j).start()
+
+    def core_done(self):
+        for j in self.order:
+            self.core_copy(j).wait_recv()
+            self.acc[j] = self.g[self.there(j), self.core] + self.fromcore[j]
             if j:
-                chip_copy(k, j).start()
-    for k in range(count):
-        acc, fromchip = parts(k)[1:3]
-        for j in range(1, chips):
-            chip_copy(k, j).wait_recv()
-            acc[0] = acc[0] + fromchip[j]
-        for j in range(1, members):
-            line_copy(k, j).start()
-    for k in range(count):
-        acc, fromline = parts(k)[1], parts(k)[3]
-        total = acc[0, member]
-        for j in range(1, members):
-            line_copy(k, j).wait_recv()
-            total = total + fromline[j]
-        outs[k][...] = total
-    for k in range(count):
-        for j in range(chips):
-            core_copy(k, j).wait_send()
-        for j in range(1, chips):
-            chip_copy(k, j).wait_send()
-        for j in range(1, members):
-            line_copy(k, j).wait_send()
-
-
-def scatter(gs, faces, members, ident):
-    chips = faces // 2
-    scratch = []
-    for g in gs:
-        tail = g.shape[3:]
-        scratch += [
-            VMEM((chips, members) + tail, f32),
-            VMEM((chips, members) + tail, f32),
-            VMEM((chips, members) + tail, f32),
-            VMEM((members,) + tail, f32),
-        ] + dma_sems(chips, chips, chips, chips, members, members)
-    return pl.pallas_call(
-        functools.partial(scatter_kernel, chips, members, len(gs)),
-        out_shape=[jax.ShapeDtypeStruct(g.shape[3:], f32) for g in gs],
-        in_specs=[pl.BlockSpec(memory_space=VMEM)] * len(gs),
-        out_specs=[pl.BlockSpec(memory_space=VMEM)] * len(gs),
-        scratch_shapes=scratch,
-        compiler_params=pltpu.CompilerParams(
-            collective_id=ident, has_side_effects=True, vmem_limit_bytes=LIMIT
-        ),
-        name="scatter",
-    )(*gs)
+                self.chip_copy(j).start()
+
+    def chip_done(self):
+        for j in range(1, self.chips):
+            self.chip_copy(j).wait_recv()
+            self.acc[0] = self.acc[0] + self.fromchip[j]
+        for j in range(1, self.members):
+            self.line_copy(j).start()
+
+    def line_done(self):
+        total = self.acc[0, self.member]
+        for j in range(1, self.members):
+            self.line_copy(j).wait_recv()
+            total = total + self.fromline[j]
+        self.out[...] = total
+
+    def finish(self):
+        for j in range(self.chips):
+            self.core_copy(j).wait_send()
+        for j in range(1, self.chips):
+            self.chip_copy(j).wait_send()
+        for j in range(1, self.members):
+            self.line_copy(j).wait_send()
+
+
+def scatter_scratch(chips, members, tail):
+    return [
+        VMEM((chips, members) + tail, f32),
+        VMEM((chips, members) + tail, f32),
+        VMEM((chips, members) + tail, f32),
+        VMEM((members,) + tail, f32),
+    ] + dma_sems(chips, chips, chips, chips, members, members)
 
 
 def rims_of(index_ref, flip_ref, edges_ref, n, length):
@@ -773,74 +766,164 @@
     )(slope_out, act, pre, head_t, w)
 
 
-def grad_kernel(block, steps, mid, h, w, *refs):
-    if mid:
-        index_ref, flip_ref, edges_ref, inner_ref, pre_ref, x3_ref, out_ref, acc, field = refs
-    else:
-        slope_ref, x3_ref, out_ref, acc = refs
+def add_products(acc, slopes, x3_ref, h, w):
+    block, _, _, width = x3_ref.shape
+    turned = jnp.concatenate([v.T for v in slopes], axis=1)
+    for a in range(3):
+        acc[a] += mm(turned, x3_ref[:, a : a + h].reshape(block * h * w, width))
+
+
+def turn_out(acc, out_ref):
     c = out_ref.shape[-1]
+    for a in range(3):
+        for b in range(3):
+            out_ref[(3 * a + b) * c : (3 * a + b + 1) * c, :] = acc[
+                a, :, b * c : (b + 1) * c
+            ].T
+
+
+def grad_two_kernel(block, steps, chips, h, w, *refs):
+    slope_ref, x3_ref, side_ref, out_ref, sides_ref, acc, own_sem = refs[:7]
     step = pl.program_id(0)
+    gather = gather_over_face(side_ref, sides_ref, chips, refs[7:])
+    own = pltpu.make_async_copy(side_ref, sides_ref.at[lax.axis_index("face")], own_sem.at[0])
 
     @pl.when(step == 0)
     def _():
+        own.start()
+        greet(chips, 1, True, False)
+        gather.start()
+        acc[...] = jnp.zeros_like(acc)
+
+    add_products(acc, [slope_ref[k] for k in range(block)], x3_ref, h, w)
+
+    @pl.when(step == min(1, steps - 1))
+    def _():
+        gather.relay_first()
+
+    @pl.when(step == steps - 1)
+    def _():
+        turn_out(acc, out_ref)
+        own.wait()
+        gather.relay_rest()
+        gather.finish()
+
+
+def grad_two_gather(x3, slope, sides, h, w, faces, ident):
+    n, _, _, width = x3.shape
+    c = width // 3
+    block = block_of(n)
+    chips = faces // 2
+    return pl.pallas_call(
+        functools.partial(grad_two_kernel, block, n // block, chips, h, w),
+        grid=(n // block,),
+        out_shape=[
+            jax.ShapeDtypeStruct((9 * c, c), f32),
+            jax.ShapeDtypeStruct((faces,) + sides.shape, sides.dtype),
+        ],
+        in_specs=[
+            tiles(block, slope.shape[1:]),
+            tiles(block, x3.shape[1:]),
+            whole(sides.shape),
+        ],
+        out_specs=[whole((9 * c, c)), pl.BlockSpec(memory_space=pl.ANY)],
+        scratch_shapes=[VMEM((3, c, width), f32)]
+        + dma_sems(1)
+        + dma_sems(*([chips + 3] * 4)),
+        compiler_params=pltpu.CompilerParams(
+            collective_id=ident, has_side_effects=True, vmem_limit_bytes=LIMIT
+        ),
+        name="grad_two",
+    )(slope, x3, sides)
+
+
+def grad_one_kernel(block, steps, chips, members, h, w, *refs):
+    index_ref, flip_ref, edges_ref, inner_ref, pre_ref, x3_ref, two_ref, hg_ref = refs[:8]
+    one_out, two_out, hg_out, acc, field, one_flat, one = refs[8:15]
+    rest = refs[15:]
+    c = one_flat.shape[-1]
+    step = pl.program_id(0)
+    s_two = Scatter(two_ref, two_out, chips, members, rest[:10])
+    s_head = Scatter(hg_ref, hg_out, chips, members, rest[10:20])
+    s_one = Scatter(one, one_out, chips, members, rest[20:30])
+
+    @pl.when(step == 0)
+    def _():
+        greet(chips, members, True, True)
+        s_two.core_start()
+        s_head.core_start()
         acc[...] = jnp.zeros_like(acc)
 
     slopes = []
     for k in range(block):
-        if mid:
-            rims = rims_of(index_ref, flip_ref, edges_ref, step * block + k, w)
-            field[...] = inner_ref[k].astype(f32)
-            field[0] += rims[0:w]
-            field[:, w - 1 : w, :] += rims[w : w + h].reshape(h, 1, c)
-            field[h - 1] += rims[w + h : 2 * w + h]
-            field[:, 0:1, :] += rims[2 * w + h :].reshape(h, 1, c)
-            slope = (field[...].reshape(h * w, c) * dsilu(pre_ref[k])).astype(bf16)
-        else:
-            slope = slope_ref[k]
-        slopes.append(slope.T)
-    turned = jnp.concatenate(slopes, axis=1)
-    for a in range(3):
-        acc[a] += mm(turned, x3_ref[:, a : a + h].reshape(block * h * w, 3 * c))
+        rims = rims_of(index_ref, flip_ref, edges_ref, step * block + k, w)
+        field[...] = inner_ref[k].astype(f32)
+        field[0] += rims[0:w]
+        field[:, w - 1 : w, :] += rims[w : w + h].reshape(h, 1, c)
+        field[h - 1] += rims[w + h : 2 * w + h]
+        field[:, 0:1, :] += rims[2 * w + h :].reshape(h, 1, c)
+        slopes.append((field[...].reshape(h * w, c) * dsilu(pre_ref[k])).astype(bf16))
+    add_products(acc, slopes, x3_ref, h, w)
+
+    @pl.when(step == 0)
+    def _():
+        s_two.core_done()
+        s_head.core_done()
 
     @pl.when(step == steps - 1)
     def _():
-        for a in range(3):
-            for b in range(3):
-                out_ref[(3 * a + b) * c : (3 * a + b + 1) * c, :] = acc[
-                    a, :, b * c : (b + 1) * c
-                ].T
-
-
-def weight_grad(x3, h, w, c, slope=None, mid=None):
-    n = x3.shape[0]
+        turn_out(acc, one_flat)
+        rows = one.shape[3]
+        for d in range(chips * 2 * members):
+            one[d // (2 * members), d // members % 2, d % members] = one_flat[
+                d * rows : (d + 1) * rows
+            ]
+        s_one.core_start()
+        s_one.core_done()
+        s_two.chip_done()
+        s_head.chip_done()
+        s_one.chip_done()
+        s_two.line_done()
+        s_head.line_done()
+        s_one.line_done()
+        for s in (s_two, s_head, s_one):
+            s.finish()
+
+
+def grad_one_scatter(scalars, edges, inner, pre, x3, two, hg, faces, members, ident):
+    n, h, w, c = inner.shape
     block = block_of(n)
-    steps = n // block
-    scratch = [VMEM((3, c, 3 * c), f32)]
-    if mid is None:
-        args = [slope, x3]
-        in_specs = [tiles(block, slope.shape[1:]), tiles(block, x3.shape[1:])]
-    else:
-        index, flips, edges, inner, pre = mid
-        args = [index, flips, edges, inner, pre, x3]
-        in_specs = [
+    chips = faces // 2
+    tails = [two.shape[3:], hg.shape[3:], two.shape[3:]]
+    scratch = [
+        VMEM((3, c, 3 * c), f32),
+        VMEM((h, w, c), f32),
+        VMEM((9 * c, c), f32),
+        VMEM(two.shape, f32),
+    ]
+    for tail in tails:
+        scratch += scatter_scratch(chips, members, tail)
+    return pl.pallas_call(
+        functools.partial(grad_one_kernel, block, n // block, chips, members, h, w),
+        grid=(n // block,),
+        out_shape=[jax.ShapeDtypeStruct(tails[k], f32) for k in (2, 0, 1)],
+        in_specs=[
             SMEM_SPEC,
             SMEM_SPEC,
             whole(edges.shape),
             tiles(block, inner.shape[1:]),
             tiles(block, pre.shape[1:]),
             tiles(block, x3.shape[1:]),
-        ]
-        scratch.append(VMEM((h, w, c), f32))
-    return pl.pallas_call(
-        functools.partial(grad_kernel, block, steps, mid is not None, h, w),
-        grid=(steps,),
-        out_shape=jax.ShapeDtypeStruct((9 * c, c), f32),
-        in_specs=in_specs,
-        out_specs=whole((9 * c, c)),
+            whole(two.shape),
+            whole(hg.shape),
+        ],
+        out_specs=[whole(tails[k]) for k in (2, 0, 1)],
         scratch_shapes=scratch,
-        compiler_params=pltpu.CompilerParams(vmem_limit_bytes=LIMIT),
-        name="grad_two" if mid is None else "grad_one",
-    )(*args)
+        compiler_params=pltpu.CompilerParams(
+            collective_id=ident, has_side_effects=True, vmem_limit_bytes=LIMIT
+        ),
+        name="grad_one",
+    )(*scalars, edges, inner, pre, x3, two, hg)
 
 
 def shards(faces, zs, features, observed, conv_weights, head_weight, adjacency, placement_map):
@@ -869,17 +952,17 @@
     )
     slope_out = score_exchange(outs, observed, zs, h, 3)
     slope_two, inner, borders, hg = backward(slope_out, act_two, pre_two, head_t, weights, h, w)
-    grad_two = weight_grad(x3_two, h, w, c, slope=slope_two)
-    returned = flat(face_gather(borders, faces, 4))
-    grad_one = weight_grad(x3_one, h, w, c, mid=(index, flips, returned, inner, pre_one))
+    grad_two, returned = grad_two_gather(x3_two, slope_two, borders, h, w, faces, 4)
     hg = jnp.pad(hg.T, ((0, 0), (0, lanes - variables)))
     chips = faces // 2
-    one, two, head_out = scatter(
-        [
-            grad_one.reshape(chips, 2, zs, rows, c),
-            grad_two.reshape(chips, 2, zs, rows, c),
-            hg.reshape(chips, 2, zs, head_rows, lanes),
-        ],
+    one, two, head_out = grad_one_scatter(
+        (index, flips),
+        flat(returned),
+        inner,
+        pre_one,
+        x3_one,
+        grad_two.reshape(chips, 2, zs, rows, c),
+        hg.reshape(chips, 2, zs, head_rows, lanes),
         faces,
         zs,
         5,

time: 214 us -> 195 us (0.911)
  Pallas kernels: 203 us -> 184 us
    pallas_call x2 -> x1, Pallas kernels: 40.9 us -> 22 us  [face_gather(): pl.pallas_call(functools.partial(face_gather_kernel, chips), out_shape=ja...]
    pallas_call x3 -> x2, Pallas kernels: 63.8 us -> 64.1 us  [the longest x1 44.4 us: grad_one_scatter(): pl.pallas_call(functools.partial(grad_one_kernel, block, n // block, chip...]
where the time goes in v3:
time: 195 us
  Pallas kernels  184 us (94%)
  local copies, waits for them, and re-layouts  8.66 us (4%)
    pallas_call x1, Pallas kernels, grad_one_scatter(): pl.pallas_call(functools.partial(grad_one_kernel, block, n // block, chip...  44.4 us
    pallas_call x1, Pallas kernels, first_gather(): pl.pallas_call(functools.partial(first_gather_kernel, chips, members, cou...  39.4 us
    pallas_call x1, Pallas kernels, score_exchange(): pl.pallas_call(functools.partial(score_kernel, members, held, tile_dev, c...  27.8 us
    pallas_call x1, Pallas kernels, face_gather(): pl.pallas_call(functools.partial(face_gather_kernel, chips), out_shape=ja...  22 us
    pallas_call x2, Pallas kernels, conv(): pl.pallas_call(functools.partial(conv_kernel, block, members), grid=(n //...  20.4 us
    pallas_call x1, Pallas kernels, grad_two_gather(): pl.pallas_call(functools.partial(grad_two_kernel, block, n // block, chip...  19.7 us
    pallas_call x1, Pallas kernels, backward(): pl.pallas_call(functools.partial(back_kernel, block, h, wd), grid=(n // b...  10.5 us
    unnamed x13, local copies, waits for them, and re-layouts  5.92 us

profile of v3, /device:TPU:0, one launch (start us, length us, event | category | flops | bytes accessed | tf_op | source)
XLA Modules:
  0.0 194.5 jit_solution(6722595454318365692)
XLA Ops:
  0.6 1.5 copy.19
  2.2 1.3 pad.8.refs_2_
  3.4 39.4 %first_gather.1 = (bf16[8,12,4,16,256]{4,3,2,1,0:T(8,128)(2,1)}, bf16[8,4,72,512]{3,2,1,0:T(8,128)(2,1)}, bf16[8,4,8,128]{3,2,1,0:T(8,128)(2,1)}) custom-call(bf16[12,16,16,256]{3,2,1,0:T(8,128)(2,1)} %bitcast.20, bf16[72,512]{1,0:T(8,128)(2,1)} %bitcast.28, bf16[8,128]{1,0:T(8,128)(2,1)} %pad.8.refs_2_), custom_call_target="tpu_custom_call" | custom-call | tf_op jit(solution)/shard_map/first_gather/pallas_call | solution.py:284
  42.8 0.8 copy.12
  43.6 0.8 reshape.34.refs_1_
  44.4 10.8 %conv_first.1 = (bf16[12,18,16,768]{3,2,1,0:T(8,128)(2,1)}, f32[12,256,256]{2,1,0:T(8,128)}, bf16[12,16,16,256]{3,2,1,0:T(8,128)(2,1)}, bf16[12,4,16,256]{3,2,1,0:T(8,128)(2,1)}, s32[48]{0:T(128)}, /*index=5*/s32[48]{0:T(128)}) custom-call(s32[48]{0:T(128)} %refs_0_.1, s32[576]{0:T(1024)} %reshape.34.refs_1_, bf16[12,16,16,256]{3,2,1,0:T(8,128)(2,1)} %bitcast.21, ...), custom_call_target="tpu_custom_call" | custom-call | tf_op jit(solution)/shard_map/conv_first/pallas_call | solution.py:676
  55.2 0.0 copy-start.2
  55.2 22.0 %face_gather.1 = bf16[8,12,4,16,256]{4,3,2,1,0:T(8,128)(2,1)} custom-call(bf16[12,4,16,256]{3,2,1,0:T(8,128)(2,1)} %get-tuple-element.29.x), custom_call_target="tpu_custom_call" | custom-call | tf_op jit(solution)/shard_map/face_gather/pallas_call | solution.py:310
  77.2 0.0 copy-done.2
  77.2 0.7 copy.17
  78.0 0.0 copy-start
  78.0 9.6 %conv_last.1 = (bf16[12,18,16,768]{3,2,1,0:T(8,128)(2,1)}, f32[12,256,256]{2,1,0:T(8,128)}, bf16[12,256,256]{2,1,0:T(8,128)(2,1)}, bf16[12,80,256]{2,1,0:T(8,128)(2,1)}) custom-call(s32[48]{0:T(128)} %get-tuple-element.26.refs_0_, s32[48]{0:T(128)} %get-tuple-element.27.refs_1_, bf16[12,16,16,256]{3,2,1,0:T(8,128)(2,1)} %get-tuple-element.28.refs_2_, ...), custom_call_target="tpu_custom_call" | custom-call | tf_op jit(solution)/shard_map/conv_last/pallas_call | solution.py:676
  87.6 0.0 copy-done
  87.6 0.8 copy.14.refs_1_
  88.3 27.8 %score.1.refs_0_ = bf16[12,80,256]{2,1,0:T(8,128)(2,1)} custom-call(bf16[12,80,256]{2,1,0:T(8,128)(2,1)} %get-tuple-element.31.refs_0_, bf16[6,80,64]{2,1,0:T(8,128)(2,1)} %copy.14.refs_1_), custom_call_target="tpu_custom_call" | custom-call | tf_op jit(solution)/shard_map/score/pallas_call | solution.py:423
  116.1 10.5 %backward.1 = (bf16[12,256,256]{2,1,0:T(8,128)(2,1)}, bf16[12,16,16,256]{3,2,1,0:T(8,128)(2,1)}, bf16[12,4,16,256]{3,2,1,0:T(8,128)(2,1)}, f32[80,256]{1,0:T(8,128)}) custom-call(bf16[12,80,256]{2,1,0:T(8,128)(2,1)} %score.1.refs_0_, bf16[12,256,256]{2,1,0:T(8,128)(2,1)} %get-tuple-element.32.refs_1_, f32[12,256,256]{2,1,0:T(8,128)} %get-tuple-element.33.refs_2_, ...), custom_call_target="tpu_custom_call" | custom-call | tf_op jit(solution)/shard_map/backward/pallas_call | solution.py:745
  126.6 0.0 copy-start.1
  126.6 19.7 %grad_two.1 = (f32[2304,256]{1,0:T(8,128)}, bf16[8,12,4,16,256]{4,3,2,1,0:T(8,128)(2,1)}) custom-call(bf16[12,256,256]{2,1,0:T(8,128)(2,1)} %get-tuple-element.34.refs_0_, bf16[12,18,16,768]{3,2,1,0:T(8,128)(2,1)} %get-tuple-element.35.refs_1_, bf16[12,4,16,256]{3,2,1,0:T(8,128)(2,1)} %get-tuple-element.36.refs_2_), custom_call_target="tpu_custom_call" | custom-call | tf_op jit(solution)/shard_map/grad_two/pallas_call | solution.py:817
  146.4 0.0 copy-done.1
  146.4 0.1 copy.18
  146.5 0.7 pad.9.clone
  147.1 44.4 %grad_one.1 = (f32[72,256]{1,0:T(8,128)}, f32[72,256]{1,0:T(8,128)}, f32[8,128]{1,0:T(8,128)}) custom-call(s32[48]{0:T(128)} %get-tuple-element.26.refs_0_, s32[48]{0:T(128)} %get-tuple-element.27.refs_1_, bf16[384,16,256]{2,1,0:T(8,128)(2,1)} %bitcast.23, bf16[12,16,16,256]{3,2,1,0:T(8,128)(2,1)} %get-tuple-element.38.refs_3_, ...), custom_call_target="tpu_custom_call" | custom-call | tf_op jit(solution)/shard_map/grad_one/pallas_call | solution.py:906
  191.6 0.9 pad_maximum_fusion
  192.5 0.7 copy.16
  193.3 1.3 copy.21
Async XLA Ops:
  55.2 22.0 %copy-start.2 = (bf16[8,4,8,128]{3,2,1,0:T(8,128)(2,1)S(1)}, bf16[8,4,8,128]{3,2,1,0:T(8,128)(2,1)}, u32[]{:S(2)}) copy-start(bf16[8,4,8,128]{3,2,1,0:T(8,128)(2,1)} %get-tuple-element.30) | copy-start | bytes 196612
  78.0 9.6 %copy-start = (bf16[6,80,64]{1,2,0:T(8,128)(2,1)S(1)}, bf16[6,80,64]{1,2,0:T(8,128)(2,1)}, u32[]{:S(2)}) copy-start(bf16[6,80,64]{1,2,0:T(8,128)(2,1)} %param.7) | copy-start | bytes 184324
  126.6 19.7 %copy-start.1 = (f32[80,256]{1,0:T(8,128)S(1)}, f32[80,256]{1,0:T(8,128)}, u32[]{:S(2)}) copy-start(f32[80,256]{1,0:T(8,128)} %get-tuple-element.42) | copy-start | bytes 245764

commit v4 on v3

--- a/solution.py
+++ b/solution.py
@@ -235,9 +235,8 @@
     member = lax.axis_index("member")
     own = []
     for k in range(count):
-        own.append(
-            pltpu.make_async_copy(ws[k], outs[k].at[face, member], own_sem.at[k + 1])
-        )
+        place = outs[k].at[member] if k else outs[k].at[face, member]
+        own.append(pltpu.make_async_copy(ws[k], place, own_sem.at[k + 1]))
         own[k].start()
 
     def cut(k, carry):
@@ -253,21 +252,17 @@
     for c in own:
         c.wait()
     rest = sems[4:]
-    wgs = []
-    for k in range(count):
-        line = rest[8 * k : 8 * k + 4]
-        line_gather(ws[k], lambda b: outs[k].at[face, b], member, members, line)
-        wg = gather_over_face(outs[k].at[face], outs[k], chips, rest[8 * k + 4 : 8 * k + 8])
-        wg.start()
-        wgs.append(wg)
-        if k == 0:
-            eg.relay_first()
+    line_gather(ws[0], lambda b: outs[0].at[face, b], member, members, rest[:4])
+    wg = gather_over_face(outs[0].at[face], outs[0], chips, rest[4:8])
+    wg.start()
+    eg.relay_first()
+    for k in range(1, count):
+        line = rest[4 * k + 4 : 4 * k + 8]
+        line_gather(ws[k], lambda b: outs[k].at[b], member, members, line)
     eg.relay_rest()
-    for wg in wgs:
-        wg.relay()
+    wg.relay()
     eg.finish()
-    for wg in wgs:
-        wg.finish()
+    wg.finish()
 
 
 def first_gather(x, ws, faces, members):
@@ -275,12 +270,13 @@
     count = len(ws)
     n, h, w, c = x.shape
     shapes = [jax.ShapeDtypeStruct((faces, n, 4, w, c), x.dtype)] + [
-        jax.ShapeDtypeStruct((faces, members) + v.shape, v.dtype) for v in ws
+        jax.ShapeDtypeStruct((members,) + v.shape, v.dtype) for v in ws
     ]
+    shapes[1] = jax.ShapeDtypeStruct((faces,) + shapes[1].shape, shapes[1].dtype)
     scratch = [VMEM((n, 4, w, c), x.dtype), VMEM((h, w, c), f32)]
     scratch += dma_sems(count + 1) + dma_sems(*([chips + 3] * 4))
-    for _ in ws:
-        scratch += dma_sems(*([members] * 4)) + dma_sems(*([chips + 3] * 4))
+    scratch += dma_sems(*([members] * 4)) + dma_sems(*([chips + 3] * 4))
+    scratch += dma_sems(*([members] * 4)) * (count - 1)
     return pl.pallas_call(
         functools.partial(first_gather_kernel, chips, members, count),
         out_shape=shapes,
@@ -551,7 +547,7 @@
     return s * (1.0 + v * (1.0 - s))
 
 
-def table(place_ref, glue_ref, index_ref, flip_ref, slot_of, members, tile_dev):
+def table_kernel(members, tile_dev, place_ref, glue_ref, index_ref, flip_ref, slot_of):
     first = lax.axis_index("face") * tile_dev
 
     def invert(s, carry):
@@ -576,21 +572,49 @@
     lax.fori_loop(0, tile_dev, fill, 0)
 
 
-def conv_kernel(block, members, *refs):
-    last = members is None
+def edge_table(placement_map, glue, members, tile_dev):
+    size = members * tile_dev * 4
+    return pl.pallas_call(
+        functools.partial(table_kernel, members, tile_dev),
+        out_shape=[jax.ShapeDtypeStruct((size,), jnp.int32)] * 2,
+        in_specs=[SMEM_SPEC] * 2,
+        out_specs=[SMEM_SPEC] * 2,
+        scratch_shapes=[pltpu.SMEM(placement_map.shape, jnp.int32)],
+        name="table",
+    )(placement_map, glue)
+
+
+def conv_kernel(block, steps, chips, *refs):
+    last = chips is None
+    index_ref, flip_ref, x_ref, edges_ref, w_ref = refs[:5]
     if last:
-        index_ref, flip_ref, x_ref, edges_ref, w_ref = refs[:5]
         head_ref, x3_ref, pre_ref, act_ref, out_ref, pad = refs[5:]
     else:
-        place_ref, glue_ref, x_ref, edges_ref, w_ref = refs[:5]
-        x3_ref, pre_ref, act_ref, side_ref, index_ref, flip_ref, pad, field, slot_of = refs[5:]
+        late, late_out = refs[5:7], refs[11:13]
+        x3_ref, pre_ref, act_ref, side_ref = refs[7:11]
+        pad, field, own_sem = refs[13:16]
+        gathers = [
+            gather_over_face(late[k], late_out[k], chips, refs[16 + 4 * k : 20 + 4 * k])
+            for k in range(2)
+        ]
+        own = [
+            pltpu.make_async_copy(
+                late[k], late_out[k].at[lax.axis_index("face")], own_sem.at[k]
+            )
+            for k in range(2)
+        ]
     _, h, w, c = x_ref.shape
     step = pl.program_id(0)
     if not last:
-        tile_dev = index_ref.shape[0] // (4 * members)
-        pl.when(step == 0)(
-            lambda: table(place_ref, glue_ref, index_ref, flip_ref, slot_of, members, tile_dev)
-        )
+
+        @pl.when(step == 0)
+        def _():
+            for copy in own:
+                copy.start()
+            greet(chips, 1, True, False)
+            for gather in gathers:
+                gather.start()
+
     for k in range(block):
         n = step * block + k
         rims = rims_of(index_ref, flip_ref, edges_ref, n, w)
@@ -623,6 +647,20 @@
             field[...] = act[k * h * w : (k + 1) * h * w].astype(f32).reshape(h, w, c)
             sides_out(field, side_ref, k)
 
+        @pl.when(step == min(1, steps - 1))
+        def _():
+            for gather in gathers:
+                gather.relay_first()
+
+        @pl.when(step == steps - 1)
+        def _():
+            for gather in gathers:
+                gather.relay_rest()
+            for copy in own:
+                copy.wait()
+            for gather in gathers:
+                gather.finish()
+
 
 def whole(shape):
     return pl.BlockSpec(shape, lambda i: (0,) * len(shape))
@@ -639,20 +677,17 @@
     return 3 if n % 3 == 0 else (2 if n % 2 == 0 else 1)
 
 
-def layer(shape, which):
-    return pl.BlockSpec((shape[0], shape[1] // 2), lambda i: (0, which))
-
-
-def conv(scalars, x, edges, w, members=None, head_t=None):
+def conv(scalars, x, edges, w, faces=None, late=None, head_t=None):
     n, h, wd, c = x.shape
     block = block_of(n)
-    last = members is None
+    last = head_t is not None
+    chips = None if last else faces // 2
     in_specs = [
         SMEM_SPEC,
         SMEM_SPEC,
         tiles(block, (h, wd, c)),
         whole(edges.shape),
-        layer(w.shape, int(last)),
+        whole(w.shape),
     ]
     shapes = [
         jax.ShapeDtypeStruct((n, h + 2, wd, 3 * c), bf16),
@@ -661,26 +696,30 @@
     ]
     args = [*scalars, x, edges, w]
     scratch = [VMEM((h + 2, wd + 16, c), f32)]
+    extra = {}
     if last:
         in_specs.append(whole(head_t.shape))
         args.append(head_t)
         shapes.append(jax.ShapeDtypeStruct((n, head_t.shape[0], h * wd), bf16))
     else:
+        in_specs += [whole(v.shape) for v in late]
+        args += late
         shapes.append(jax.ShapeDtypeStruct((n, 4, wd, c), bf16))
         scratch.append(VMEM((h, wd, c), f32))
-        scratch.append(pltpu.SMEM(scalars[0].shape, jnp.int32))
+        scratch += dma_sems(2) + dma_sems(*([chips + 3] * 8))
+        extra = dict(collective_id=6, has_side_effects=True)
     out_specs = [tiles(block, s.shape[1:]) for s in shapes]
     if not last:
-        shapes += [jax.ShapeDtypeStruct((n * 4,), jnp.int32)] * 2
-        out_specs += [SMEM_SPEC] * 2
+        shapes += [jax.ShapeDtypeStruct((faces,) + v.shape, v.dtype) for v in late]
+        out_specs += [pl.BlockSpec(memory_space=pl.ANY)] * 2
     return pl.pallas_call(
-        functools.partial(conv_kernel, block, members),
+        functools.partial(conv_kernel, block, n // block, chips),
         grid=(n // block,),
         out_shape=shapes,
         in_specs=in_specs,
         out_specs=out_specs,
         scratch_shapes=scratch,
-        compiler_params=pltpu.CompilerParams(vmem_limit_bytes=LIMIT),
+        compiler_params=pltpu.CompilerParams(vmem_limit_bytes=LIMIT, **extra),
         name="conv_last" if last else "conv_first",
     )(*args)
 
@@ -751,7 +790,7 @@
             tiles(block, (cells, c)),
             tiles(block, (cells, c)),
             whole(head_t.shape),
-            layer(w.shape, 1),
+            whole(w.shape),
         ],
         out_specs=[tiles(block, s.shape[1:]) for s in shapes[:3]] + [whole(head_t.shape)],
         scratch_shapes=[
@@ -935,23 +974,26 @@
     head_rows = head_weight.shape[0]
     lanes = -(-variables // 128) * 128
     head_wide = jnp.pad(head_weight, ((0, 0), (0, lanes - variables)))
-    edges, weights, head = first_gather(
-        x, [conv_weights.reshape(rows, 2 * c), head_wide], faces, zs
+    edges, w0, w1_line, head_line = first_gather(
+        x, [conv_weights[:, 0], conv_weights[:, 1], head_wide], faces, zs
     )
-    weights = weights.reshape(faces * zs * rows, 2 * c)
-    head_t = head.reshape(faces * zs * head_rows, lanes)[:, :variables].T
+    w0 = w0.reshape(faces * zs * rows, c)
 
     def flat(e):
         return e.reshape((faces * n * 4,) + e.shape[-2:])
 
-    x3_one, pre_one, act_one, sides, index, flips = conv(
-        (placement_map, adjacency.reshape(-1)), x, flat(edges), weights, members=members
+    scalars = edge_table(placement_map, adjacency.reshape(-1), members, tile_dev)
+    index, flips = scalars
+    x3_one, pre_one, act_one, sides, w1, head = conv(
+        scalars, x, flat(edges), w0, faces=faces, late=[w1_line, head_line]
     )
+    w1 = w1.reshape(faces * zs * rows, c)
+    head_t = head.reshape(faces * zs * head_rows, lanes)[:, :variables].T
     x3_two, pre_two, act_two, outs = conv(
-        (index, flips), act_one, flat(face_gather(sides, faces, 2)), weights, head_t=head_t
+        scalars, act_one, flat(face_gather(sides, faces, 2)), w1, head_t=head_t
     )
     slope_out = score_exchange(outs, observed, zs, h, 3)
-    slope_two, inner, borders, hg = backward(slope_out, act_two, pre_two, head_t, weights, h, w)
+    slope_two, inner, borders, hg = backward(slope_out, act_two, pre_two, head_t, w1, h, w)
     grad_two, returned = grad_two_gather(x3_two, slope_two, borders, h, w, faces, 4)
     hg = jnp.pad(hg.T, ((0, 0), (0, lanes - variables)))
     chips = faces // 2

time: 195 us -> 203 us (1.041)
  Pallas kernels: 184 us -> 191 us
    pallas_call x2 -> x3, Pallas kernels: 20.4 us -> 28.5 us  [the longest x2 26.4 us: conv(): pl.pallas_call(functools.partial(conv_kernel, block, n // block, chips),...]
    unnamed x13 -> x10, local copies, waits for them, and re-layouts: 5.92 us -> 5.24 us
where the time goes in v4:
time: 203 us
  Pallas kernels  191 us (94%)
  local copies, waits for them, and re-layouts  9.71 us (5%)
    pallas_call x1, Pallas kernels, grad_one_scatter(): pl.pallas_call(functools.partial(grad_one_kernel, block, n // block, chip...  43.7 us
    pallas_call x1, Pallas kernels, first_gather(): pl.pallas_call(functools.partial(first_gather_kernel, chips, members, cou...  40.3 us
    pallas_call x1, Pallas kernels, score_exchange(): pl.pallas_call(functools.partial(score_kernel, members, held, tile_dev, c...  27.8 us
    pallas_call x2, Pallas kernels, conv(): pl.pallas_call(functools.partial(conv_kernel, block, n // block, chips),...  26.4 us
    pallas_call x1, Pallas kernels, grad_two_gather(): pl.pallas_call(functools.partial(grad_two_kernel, block, n // block, chip...  20.5 us
    pallas_call x1, Pallas kernels, face_gather(): pl.pallas_call(functools.partial(face_gather_kernel, chips), out_shape=ja...  20.1 us
    pallas_call x1, Pallas kernels, backward(): pl.pallas_call(functools.partial(back_kernel, block, h, wd), grid=(n // b...  10.5 us
    unnamed x10, local copies, waits for them, and re-layouts  5.24 us

profile of v4, /device:TPU:0, one launch (start us, length us, event | category | flops | bytes accessed | tf_op | source)
XLA Modules:
  0.0 202.7 jit_solution(5225691704100703095)
XLA Ops:
  0.6 1.1 fusion
  1.7 0.6 copy_bitcast_fusion
  2.4 1.3 pad.8.refs_3_
  3.6 40.3 %first_gather.1 = (bf16[8,12,4,16,256]{4,3,2,1,0:T(8,128)(2,1)}, bf16[8,4,72,256]{3,2,1,0:T(8,128)(2,1)}, bf16[4,72,256]{2,1,0:T(8,128)(2,1)}, bf16[4,8,128]{2,1,0:T(8,128)(2,1)}) custom-call(bf16[12,16,16,256]{3,2,1,0:T(8,128)(2,1)} %bitcast.20, bf16[72,256]{1,0:T(8,128)(2,1)} %get-tuple-element.59.refs_1_, bf16[72,256]{1,0:T(8,128)(2,1)} %get-tuple-element.58.refs_2_, ...), custom_call_target="tpu_custom_call" | custom-call | tf_op jit(solution)/shard_map/first_gather/pallas_call | solution.py:280
  43.9 0.8 copy.14
  44.7 0.8 reshape.34.glue_ref
  45.5 2.1 %table.1 = (s32[48]{0:T(128)}, s32[48]{0:T(128)}) custom-call(s32[48]{0:T(128)} %place_ref.1, s32[576]{0:T(1024)} %reshape.34.glue_ref), custom_call_target="tpu_custom_call" | custom-call | tf_op jit(solution)/shard_map/table/pallas_call | solution.py:577
  47.6 16.7 %conv_first.1 = (bf16[12,18,16,768]{3,2,1,0:T(8,128)(2,1)}, f32[12,256,256]{2,1,0:T(8,128)}, bf16[12,16,16,256]{3,2,1,0:T(8,128)(2,1)}, bf16[12,4,16,256]{3,2,1,...) custom-call(s32[48]{0:T(128)} %get-tuple-element.27.refs_0_, ...), custom_call_target="tpu_custom_call" | custom-call | tf_op jit(solution)/shard_map/conv_first/pallas_call | solution.py:715
  64.4 1.5 copy.23
  65.9 20.1 %face_gather.1 = bf16[8,12,4,16,256]{4,3,2,1,0:T(8,128)(2,1)} custom-call(bf16[12,4,16,256]{3,2,1,0:T(8,128)(2,1)} %get-tuple-element.34.x), custom_call_target="tpu_custom_call" | custom-call | tf_op jit(solution)/shard_map/face_gather/pallas_call | solution.py:306
  86.1 0.0 copy-start
  86.1 9.6 %conv_last.1 = (bf16[12,18,16,768]{3,2,1,0:T(8,128)(2,1)}, f32[12,256,256]{2,1,0:T(8,128)}, bf16[12,256,256]{2,1,0:T(8,128)(2,1)}, bf16[12,80,256]{2,1,0:T(8,128)(2,1)}) custom-call(s32[48]{0:T(128)} %get-tuple-element.27.refs_0_, s32[48]{0:T(128)} %get-tuple-element.28.refs_1_, bf16[12,16,16,256]{3,2,1,0:T(8,128)(2,1)} %get-tuple-element.33.refs_2_, ...), custom_call_target="tpu_custom_call" | custom-call | tf_op jit(solution)/shard_map/conv_last/pallas_call | solution.py:715
  95.7 0.0 copy-done
  95.7 0.8 copy.18.refs_1_
  96.5 27.8 %score.1.refs_0_ = bf16[12,80,256]{2,1,0:T(8,128)(2,1)} custom-call(bf16[12,80,256]{2,1,0:T(8,128)(2,1)} %get-tuple-element.37.refs_0_, bf16[6,80,64]{2,1,0:T(8,128)(2,1)} %copy.18.refs_1_), custom_call_target="tpu_custom_call" | custom-call | tf_op jit(solution)/shard_map/score/pallas_call | solution.py:419
  124.3 10.5 %backward.1 = (bf16[12,256,256]{2,1,0:T(8,128)(2,1)}, bf16[12,16,16,256]{3,2,1,0:T(8,128)(2,1)}, bf16[12,4,16,256]{3,2,1,0:T(8,128)(2,1)}, f32[80,256]{1,0:T(8,128)}) custom-call(bf16[12,80,256]{2,1,0:T(8,128)(2,1)} %score.1.refs_0_, bf16[12,256,256]{2,1,0:T(8,128)(2,1)} %get-tuple-element.38.refs_1_, f32[12,256,256]{2,1,0:T(8,128)} %get-tuple-element.39.refs_2_, ...), custom_call_target="tpu_custom_call" | custom-call | tf_op jit(solution)/shard_map/backward/pallas_call | solution.py:784
  134.8 0.0 copy-start.1
  134.8 20.5 %grad_two.1 = (f32[2304,256]{1,0:T(8,128)}, bf16[8,12,4,16,256]{4,3,2,1,0:T(8,128)(2,1)}) custom-call(bf16[12,256,256]{2,1,0:T(8,128)(2,1)} %get-tuple-element.40.refs_0_, bf16[12,18,16,768]{3,2,1,0:T(8,128)(2,1)} %get-tuple-element.41.refs_1_, bf16[12,4,16,256]{3,2,1,0:T(8,128)(2,1)} %get-tuple-element.42.refs_2_), custom_call_target="tpu_custom_call" | custom-call | tf_op jit(solution)/shard_map/grad_two/pallas_call | solution.py:856
  155.3 0.0 copy-done.1
  155.3 0.1 copy.24
  155.4 0.7 pad.9.clone
  156.1 43.7 %grad_one.1 = (f32[72,256]{1,0:T(8,128)}, f32[72,256]{1,0:T(8,128)}, f32[8,128]{1,0:T(8,128)}) custom-call(s32[48]{0:T(128)} %get-tuple-element.27.refs_0_, s32[48]{0:T(128)} %get-tuple-element.28.refs_1_, bf16[384,16,256]{2,1,0:T(8,128)(2,1)} %bitcast.25, bf16[12,16,16,256]{3,2,1,0:T(8,128)(2,1)} %get-tuple-element.44.refs_3_, ...), custom_call_target="tpu_custom_call" | custom-call | tf_op jit(solution)/shard_map/grad_one/pallas_call | solution.py:945
  199.8 0.9 pad_maximum_fusion
  200.7 0.7 copy.20
  201.5 1.3 copy.28
Async XLA Ops:
  86.1 9.6 %copy-start = (bf16[6,80,64]{1,2,0:T(8,128)(2,1)S(1)}, bf16[6,80,64]{1,2,0:T(8,128)(2,1)}, u32[]{:S(2)}) copy-start(bf16[6,80,64]{1,2,0:T(8,128)(2,1)} %param.7) | copy-start | bytes 184324
  134.8 20.5 %copy-start.1 = (f32[80,256]{1,0:T(8,128)S(1)}, f32[80,256]{1,0:T(8,128)}, u32[]{:S(2)}) copy-start(f32[80,256]{1,0:T(8,128)} %get-tuple-element.48) | copy-start | bytes 245764
